TPU v7x, 32 devices: a whole 2x2x4 slice. The times are simulated.
32 devices in a mesh: ctx: 4 (over y, core), fsdp: 8 (over z, x).
Axes of the slice: x: 2, y: 2, z: 4, core: 2. Of those that a mesh axis runs over, the one named last changes fastest.
Arguments:
- tokens: bfloat16 [8, 1024, 768], P('fsdp', 'ctx')
- cotangent: bfloat16 [8, 1024, 768], P('fsdp', 'ctx'), may hold values from -6 to 6
- lengths: int32 [8], P('fsdp'), may hold values from 512 to 1024, as said below
- w_query: float32 [768, 768], P('fsdp'), may hold values from -0.5 to 0.5
- w_key: float32 [768, 768], P('fsdp'), may hold values from -0.5 to 0.5
- w_value: float32 [768, 768], P('fsdp'), may hold values from -0.21875 to 0.21875
- w_out: float32 [768, 768], P('fsdp'), may hold values from -0.21875 to 0.21875
- w_up: float32 [768, 3072], P('fsdp'), may hold values from -0.21875 to 0.21875
- w_down: float32 [3072, 768], P('fsdp'), may hold values from -0.109375 to 0.109375
- b_query: float32 [768], P('fsdp'), may hold values from -6 to 6
- b_value: float32 [768], P('fsdp'), may hold values from -1.75 to 1.75
- b_out: float32 [768], P('fsdp'), may hold values from -1.75 to 1.75
- b_up: float32 [3072], P('fsdp'), may hold values from -1.75 to 1.75
- b_down: float32 [768], P('fsdp'), may hold values from -1.75 to 1.75
- gain_first: float32 [768], P('fsdp'), may hold values from 0.25 to 1.75
- shift_first: float32 [768], P('fsdp'), may hold values from -1.75 to 1.75
- gain_second: float32 [768], P('fsdp'), may hold values from 0.25 to 1.75
- shift_second: float32 [768], P('fsdp'), may hold values from -1.75 to 1.75
- conv_taps: float32 [12, 33], replicated, may hold values from -1 to 1
Outputs:
- output: bfloat16 [8, 1024, 768], P('fsdp', 'ctx')
- input_grad: bfloat16 [8, 1024, 768], P('fsdp', 'ctx')
- grad_w_query: float32 [768, 768], P('fsdp')
- grad_w_key: float32 [768, 768], P('fsdp')
- grad_w_value: float32 [768, 768], P('fsdp')
- grad_w_out: float32 [768, 768], P('fsdp')
- grad_w_up: float32 [768, 3072], P('fsdp')
- grad_w_down: float32 [3072, 768], P('fsdp')
- grad_b_query: float32 [768], P('fsdp')
- grad_b_value: float32 [768], P('fsdp')
- grad_b_out: float32 [768], P('fsdp')
- grad_b_up: float32 [3072], P('fsdp')
- grad_b_down: float32 [768], P('fsdp')
- grad_gain_first: float32 [768], P('fsdp')
- grad_shift_first: float32 [768], P('fsdp')
- grad_gain_second: float32 [768], P('fsdp')
- grad_shift_second: float32 [768], P('fsdp')
- grad_conv_taps: float32 [12, 33], replicated
Inputs may be any that keep to these rules, and one draw needn't show every extreme that they name: The first lengths[s] slots of sequence s are valid, the rest padding; some sequence fills all 1024 slots.
All inputs are finite; a program needn't handle non-finite values.
Results may differ from a plain program's by a relative error of at most 0.025.
The roundings to bfloat16 on the way count: a program that leaves them out, or rounds other values in their place, can miss the bound.
Values may be sent and summed in bfloat16 or wider, within the bound.
No kernel may reach another device: no remote copies, remote signals or barrier semaphores. Data moves between devices by JAX's collectives and lax.ppermute only.
A program may use at most 192 MiB of HBM per device.

v0:
```python
from functools import partial

import jax
import jax.numpy as jnp
from jax import lax
from jax.sharding import PartitionSpec as P

D = 768
HEADS = 12
HEAD_DIM = 64
LAND = 64
KSIZE = 33
ITERS = 6
HALF = 16


highest = lax.Precision.HIGHEST
norm_eps = 1e-05
masked_score = -1e30


def with_halo(block, sides, width):
    for axis, dim in sides:
        count = lax.axis_size(axis)
        forward = [(i, i + 1) for i in range(count - 1)]
        backward = [(target, source) for source, target in forward]
        low = lax.ppermute(
            lax.slice_in_dim(block, block.shape[dim] - width, None, axis=dim), axis, forward
        )
        high = lax.ppermute(lax.slice_in_dim(block, 0, width, axis=dim), axis, backward)
        block = jnp.concatenate([low, block, high], axis=dim)
    return block


def layer_norm(features, weight_gain, weight_shift):
    average = jnp.mean(features, axis=-1, keepdims=True)
    centered = features - average
    spread = jnp.mean(centered * centered, axis=-1, keepdims=True)
    return centered * lax.rsqrt(spread + norm_eps) * weight_gain + weight_shift


def newton_inverse(kernel):
    column_top = jnp.max(jnp.sum(kernel, axis=1), axis=-1)
    row_top = jnp.max(jnp.sum(kernel, axis=2), axis=-1)
    approx = jnp.swapaxes(kernel, 1, 2) / (column_top * row_top)[:, None, None]
    identity = jnp.eye(kernel.shape[1], dtype=kernel.dtype)
    for iteration in range(ITERS):
        product = jnp.einsum("hij,hjk->hik", kernel, approx, precision=highest)
        factor = 7.0 * identity - product
        factor = 15.0 * identity - jnp.einsum("hij,hjk->hik", product, factor, precision=highest)
        factor = 13.0 * identity - jnp.einsum("hij,hjk->hik", product, factor, precision=highest)
        approx = 0.25 * jnp.einsum("hij,hjk->hik", approx, factor, precision=highest)
    return approx


def landmark_inverse(land_query, land_keys):
    query_heads = land_query.reshape(LAND, HEADS, HEAD_DIM)
    key_heads = land_keys.reshape(LAND, HEADS, HEAD_DIM)
    scores = jnp.einsum("ihe,jhe->hij", query_heads, key_heads, precision=highest)
    return newton_inverse(jax.nn.softmax(scores, axis=-1))


def conv_apply(padded, taps, count):
    padded_heads = padded.reshape(padded.shape[0], HEADS, HEAD_DIM)
    summed = jnp.zeros((count, HEADS, HEAD_DIM), jnp.float32)
    for offset in range(KSIZE):
        summed = summed + taps[:, offset][None, :, None] * padded_heads[offset : offset + count]
    return summed


def conv_transpose(padded, taps, count):
    padded_heads = padded.reshape(padded.shape[0], HEADS, HEAD_DIM)
    summed = jnp.zeros((count, HEADS, HEAD_DIM), jnp.float32)
    for offset in range(KSIZE):
        begin = KSIZE - 1 - offset
        summed = summed + taps[:, offset][None, :, None] * padded_heads[begin : begin + count]
    return summed


def per_device(
    tokens,
    cotangent,
    lengths,
    w_query,
    w_key,
    w_value,
    w_out,
    w_up,
    w_down,
    b_query,
    b_value,
    b_out,
    b_up,
    b_down,
    gain_first,
    shift_first,
    gain_second,
    shift_second,
    conv_taps,
):
    gathered = (
        lax.all_gather(w_query.astype(jnp.bfloat16), "fsdp", axis=0, tiled=True),
        lax.all_gather(w_key.astype(jnp.bfloat16), "fsdp", axis=0, tiled=True),
        lax.all_gather(w_value.astype(jnp.bfloat16), "fsdp", axis=0, tiled=True),
        lax.all_gather(w_out.astype(jnp.bfloat16), "fsdp", axis=0, tiled=True),
        lax.all_gather(w_up.astype(jnp.bfloat16), "fsdp", axis=0, tiled=True),
        lax.all_gather(w_down.astype(jnp.bfloat16), "fsdp", axis=0, tiled=True),
        lax.all_gather(b_query.astype(jnp.bfloat16), "fsdp", axis=0, tiled=True),
        lax.all_gather(b_value.astype(jnp.bfloat16), "fsdp", axis=0, tiled=True),
        lax.all_gather(b_out.astype(jnp.bfloat16), "fsdp", axis=0, tiled=True),
        lax.all_gather(b_up.astype(jnp.bfloat16), "fsdp", axis=0, tiled=True),
        lax.all_gather(b_down.astype(jnp.bfloat16), "fsdp", axis=0, tiled=True),
        lax.all_gather(gain_first.astype(jnp.bfloat16), "fsdp", axis=0, tiled=True),
        lax.all_gather(shift_first.astype(jnp.bfloat16), "fsdp", axis=0, tiled=True),
        lax.all_gather(gain_second.astype(jnp.bfloat16), "fsdp", axis=0, tiled=True),
        lax.all_gather(shift_second.astype(jnp.bfloat16), "fsdp", axis=0, tiled=True),
    )
    (
        query_weight,
        key_weight,
        value_weight,
        out_weight,
        up_weight,
        down_weight,
        query_bias,
        value_bias,
        out_bias,
        up_bias,
        down_bias,
        first_gain,
        first_shift,
        second_gain,
        second_shift,
    ) = gathered
    inputs = tokens[0]
    length = lengths[0]
    own_rows = inputs.shape[0]
    groups = lax.axis_size("ctx")
    ctx_index = lax.axis_index("ctx")
    position = ctx_index * own_rows + jnp.arange(own_rows, dtype=jnp.int32)
    is_live = position < length
    valid = is_live.astype(jnp.float32)[:, None]
    landmark_ids = jnp.arange(LAND, dtype=jnp.int32)
    seg_table = (
        (position[None, :] * LAND // length == landmark_ids[:, None]) & is_live[None, :]
    ).astype(jnp.bfloat16)
    bounds = (jnp.arange(LAND + 1, dtype=jnp.int32) * length + LAND - 1) // LAND
    counts = (bounds[1:] - bounds[:-1]).astype(jnp.float32)[:, None]
    queries = (
        (jnp.dot(inputs, query_weight, preferred_element_type=jnp.float32) + query_bias)
        * valid
        * 0.125
    ).astype(jnp.bfloat16)
    keys_low = (jnp.dot(inputs, key_weight, preferred_element_type=jnp.float32) * valid).astype(
        jnp.bfloat16
    )
    values = (
        (jnp.dot(inputs, value_weight, preferred_element_type=jnp.float32) + value_bias) * valid
    ).astype(jnp.bfloat16)
    padded_values = with_halo(values, (("ctx", 0),), HALF)
    land_sums = lax.psum(
        (
            jnp.dot(seg_table, queries, preferred_element_type=jnp.float32),
            jnp.dot(seg_table, keys_low, preferred_element_type=jnp.float32),
        ),
        "ctx",
    )
    land_query = land_sums[0] / counts
    land_keys = land_sums[1] / counts
    inverse, inverse_back = jax.vjp(landmark_inverse, land_query, land_keys)
    query_heads = queries.reshape(own_rows, HEADS, HEAD_DIM)
    land_keys_low = land_keys.astype(jnp.bfloat16).reshape(LAND, HEADS, HEAD_DIM)
    land_query_low = land_query.astype(jnp.bfloat16).reshape(LAND, HEADS, HEAD_DIM)
    scores_one = jnp.einsum(
        "the,jhe->htj", query_heads, land_keys_low, preferred_element_type=jnp.float32
    )
    kernel_one = jax.nn.softmax(scores_one, axis=-1)
    kernel_one_low = kernel_one.astype(jnp.bfloat16)
    all_keys, all_values = (
        lax.all_gather(keys_low, "ctx", axis=0, tiled=True),
        lax.all_gather(values, "ctx", axis=0, tiled=True),
    )
    slot_count = own_rows * groups
    key_live = jnp.arange(slot_count, dtype=jnp.int32) < length
    key_heads = all_keys.reshape(slot_count, HEADS, HEAD_DIM)
    value_heads = all_values.reshape(slot_count, HEADS, HEAD_DIM)
    scores_three = jnp.einsum(
        "ihe,the->hit", land_query_low, key_heads, preferred_element_type=jnp.float32
    )
    scores_three = jnp.where(key_live, scores_three, masked_score)
    kernel_three = jax.nn.softmax(scores_three, axis=-1)
    kernel_three_low = kernel_three.astype(jnp.bfloat16)
    context = jnp.einsum(
        "hit,the->hie", kernel_three_low, value_heads, preferred_element_type=jnp.float32
    )
    mixing = jnp.einsum("hij,hje->hie", inverse, context, precision=highest)
    mixing_low = mixing.astype(jnp.bfloat16)
    attention = jnp.einsum(
        "htj,hje->the", kernel_one_low, mixing_low, preferred_element_type=jnp.float32
    )
    conv_out = conv_apply(padded_values, conv_taps, own_rows)
    mixed_low = (attention + conv_out).reshape(own_rows, D).astype(jnp.bfloat16)
    mixer_out = jnp.dot(mixed_low, out_weight, preferred_element_type=jnp.float32) + out_bias
    hidden, first_back = jax.vjp(
        layer_norm,
        inputs.astype(jnp.float32) + mixer_out,
        first_gain.astype(jnp.float32),
        first_shift.astype(jnp.float32),
    )
    hidden_low = hidden.astype(jnp.bfloat16)
    lifted = jnp.dot(hidden_low, up_weight, preferred_element_type=jnp.float32) + up_bias
    active, gelu_back = jax.vjp(partial(jax.nn.gelu, approximate=False), lifted)
    active_low = active.astype(jnp.bfloat16)
    feed_out = jnp.dot(active_low, down_weight, preferred_element_type=jnp.float32) + down_bias
    normed, second_back = jax.vjp(
        layer_norm,
        hidden + feed_out,
        second_gain.astype(jnp.float32),
        second_shift.astype(jnp.float32),
    )
    output = (normed * valid).astype(jnp.bfloat16)
    back_query, back_key, back_value, back_out, back_up, back_down = (
        lax.all_gather(w_query.astype(jnp.bfloat16), "fsdp", axis=0, tiled=True),
        lax.all_gather(w_key.astype(jnp.bfloat16), "fsdp", axis=0, tiled=True),
        lax.all_gather(w_value.astype(jnp.bfloat16), "fsdp", axis=0, tiled=True),
        lax.all_gather(w_out.astype(jnp.bfloat16), "fsdp", axis=0, tiled=True),
        lax.all_gather(w_up.astype(jnp.bfloat16), "fsdp", axis=0, tiled=True),
        lax.all_gather(w_down.astype(jnp.bfloat16), "fsdp", axis=0, tiled=True),
    )
    grad_normed = cotangent[0].astype(jnp.float32) * valid
    d_second, grad_second_gain, grad_second_shift = second_back(grad_normed)
    d_feed = d_second.astype(jnp.bfloat16)
    grad_down = jnp.einsum("tf,td->fd", active_low, d_feed, preferred_element_type=jnp.float32)
    grad_down_bias = jnp.sum(d_feed.astype(jnp.float32), axis=0)
    (d_active,) = gelu_back(
        jnp.einsum("td,fd->tf", d_feed, back_down, preferred_element_type=jnp.float32)
    )
    d_lifted = d_active.astype(jnp.bfloat16)
    grad_up = jnp.einsum("td,tf->df", hidden_low, d_lifted, preferred_element_type=jnp.float32)
    grad_up_bias = jnp.sum(d_lifted.astype(jnp.float32), axis=0)
    d_hidden = (
        jnp.einsum("tf,df->td", d_lifted, back_up, preferred_element_type=jnp.float32) + d_second
    )
    d_first, grad_first_gain, grad_first_shift = first_back(d_hidden)
    d_mixer = d_first.astype(jnp.bfloat16)
    grad_out = jnp.einsum("td,te->de", mixed_low, d_mixer, preferred_element_type=jnp.float32)
    grad_out_bias = jnp.sum(d_mixer.astype(jnp.float32), axis=0)
    d_mixed = jnp.einsum("te,de->td", d_mixer, back_out, preferred_element_type=jnp.float32).astype(
        jnp.bfloat16
    )
    d_mixed_heads = d_mixed.reshape(own_rows, HEADS, HEAD_DIM)
    mix_grad_part = jnp.einsum(
        "htj,the->hje", kernel_one_low, d_mixed_heads, preferred_element_type=jnp.float32
    )
    d_kernel_one = jnp.einsum(
        "the,hje->htj", d_mixed_heads, mixing_low, preferred_element_type=jnp.float32
    )
    d_scores_one = (
        kernel_one * (d_kernel_one - jnp.sum(kernel_one * d_kernel_one, axis=-1, keepdims=True))
    ).astype(jnp.bfloat16)
    d_query_heads = jnp.einsum(
        "htj,jhe->the", d_scores_one, land_keys_low, preferred_element_type=jnp.float32
    )
    land_keys_part = jnp.einsum(
        "htj,the->jhe", d_scores_one, query_heads, preferred_element_type=jnp.float32
    ).reshape(LAND, D)
    mix_grad, land_keys_sum = (
        lax.psum(mix_grad_part.astype(jnp.bfloat16), "ctx").astype(jnp.float32),
        lax.psum(land_keys_part.astype(jnp.bfloat16), "ctx").astype(jnp.float32),
    )
    d_inverse = jnp.einsum("hie,hje->hij", mix_grad, context, precision=highest)
    d_context_low = jnp.einsum("hij,hie->hje", inverse, mix_grad, precision=highest).astype(
        jnp.bfloat16
    )
    d_land_query_core, d_land_keys_core = inverse_back(d_inverse)
    d_kernel_three = jnp.einsum(
        "hie,the->hit", d_context_low, value_heads, preferred_element_type=jnp.float32
    )
    row_delta = jnp.sum(kernel_three * d_kernel_three, axis=-1, keepdims=True)
    d_scores_three = (kernel_three * (d_kernel_three - row_delta)).astype(jnp.bfloat16)
    d_land_query_three = jnp.einsum(
        "hit,the->ihe", d_scores_three, key_heads, preferred_element_type=jnp.float32
    )
    start = ctx_index * own_rows
    own_scores = lax.dynamic_slice_in_dim(d_scores_three, start, own_rows, 2)
    own_kernel = lax.dynamic_slice_in_dim(kernel_three_low, start, own_rows, 2)
    d_keys_three = jnp.einsum(
        "hit,ihe->the", own_scores, land_query_low, preferred_element_type=jnp.float32
    )
    d_values_three = jnp.einsum(
        "hit,hie->the", own_kernel, d_context_low, preferred_element_type=jnp.float32
    )
    padded_grads = with_halo(d_mixed, (("ctx", 0),), HALF)
    d_values_conv = conv_transpose(padded_grads, conv_taps, own_rows)
    value_windows = padded_values.reshape(padded_values.shape[0], HEADS, HEAD_DIM)
    taps_local = jnp.stack(
        [
            jnp.einsum(
                "the,the->h",
                d_mixed_heads,
                value_windows[offset : offset + own_rows],
                preferred_element_type=jnp.float32,
            )
            for offset in range(KSIZE)
        ],
        axis=1,
    )
    grad_taps = lax.psum(taps_local, ("ctx", "fsdp"))
    d_land_query = d_land_query_core + d_land_query_three.reshape(LAND, D)
    d_land_keys = land_keys_sum + d_land_keys_core
    table_float = seg_table.astype(jnp.float32)
    spread_query = jnp.einsum("jt,jd->td", table_float, d_land_query / counts, precision=highest)
    spread_keys = jnp.einsum("jt,jd->td", table_float, d_land_keys / counts, precision=highest)
    query_scale = (valid * 0.125).astype(jnp.bfloat16)
    valid_low = valid.astype(jnp.bfloat16)
    d_queries = (d_query_heads.reshape(own_rows, D) + spread_query).astype(
        jnp.bfloat16
    ) * query_scale
    d_keys = (d_keys_three.reshape(own_rows, D) + spread_keys).astype(jnp.bfloat16) * valid_low
    d_values = (d_values_three + d_values_conv).reshape(own_rows, D).astype(
        jnp.bfloat16
    ) * valid_low
    grad_query = jnp.einsum("td,te->de", inputs, d_queries, preferred_element_type=jnp.float32)
    grad_query_bias = jnp.sum(d_queries.astype(jnp.float32), axis=0)
    grad_key = jnp.einsum("td,te->de", inputs, d_keys, preferred_element_type=jnp.float32)
    grad_value = jnp.einsum("td,te->de", inputs, d_values, preferred_element_type=jnp.float32)
    grad_value_bias = jnp.sum(d_values.astype(jnp.float32), axis=0)
    d_inputs = (
        d_first
        + jnp.einsum("te,de->td", d_queries, back_query, preferred_element_type=jnp.float32)
        + jnp.einsum("te,de->td", d_keys, back_key, preferred_element_type=jnp.float32)
        + jnp.einsum("te,de->td", d_values, back_value, preferred_element_type=jnp.float32)
    )
    input_grad = (d_inputs * valid).astype(jnp.bfloat16)
    shares = (
        lax.psum_scatter(
            grad_query.astype(jnp.bfloat16), "fsdp", scatter_dimension=0, tiled=True
        ).astype(jnp.float32),
        lax.psum_scatter(
            grad_key.astype(jnp.bfloat16), "fsdp", scatter_dimension=0, tiled=True
        ).astype(jnp.float32),
        lax.psum_scatter(
            grad_value.astype(jnp.bfloat16), "fsdp", scatter_dimension=0, tiled=True
        ).astype(jnp.float32),
        lax.psum_scatter(
            grad_out.astype(jnp.bfloat16), "fsdp", scatter_dimension=0, tiled=True
        ).astype(jnp.float32),
        lax.psum_scatter(
            grad_up.astype(jnp.bfloat16), "fsdp", scatter_dimension=0, tiled=True
        ).astype(jnp.float32),
        lax.psum_scatter(
            grad_down.astype(jnp.bfloat16), "fsdp", scatter_dimension=0, tiled=True
        ).astype(jnp.float32),
        lax.psum_scatter(
            grad_query_bias.astype(jnp.bfloat16), "fsdp", scatter_dimension=0, tiled=True
        ).astype(jnp.float32),
        lax.psum_scatter(
            grad_value_bias.astype(jnp.bfloat16), "fsdp", scatter_dimension=0, tiled=True
        ).astype(jnp.float32),
        lax.psum_scatter(
            grad_out_bias.astype(jnp.bfloat16), "fsdp", scatter_dimension=0, tiled=True
        ).astype(jnp.float32),
        lax.psum_scatter(
            grad_up_bias.astype(jnp.bfloat16), "fsdp", scatter_dimension=0, tiled=True
        ).astype(jnp.float32),
        lax.psum_scatter(
            grad_down_bias.astype(jnp.bfloat16), "fsdp", scatter_dimension=0, tiled=True
        ).astype(jnp.float32),
        lax.psum_scatter(
            grad_first_gain.astype(jnp.bfloat16), "fsdp", scatter_dimension=0, tiled=True
        ).astype(jnp.float32),
        lax.psum_scatter(
            grad_first_shift.astype(jnp.bfloat16), "fsdp", scatter_dimension=0, tiled=True
        ).astype(jnp.float32),
        lax.psum_scatter(
            grad_second_gain.astype(jnp.bfloat16), "fsdp", scatter_dimension=0, tiled=True
        ).astype(jnp.float32),
        lax.psum_scatter(
            grad_second_shift.astype(jnp.bfloat16), "fsdp", scatter_dimension=0, tiled=True
        ).astype(jnp.float32),
    )
    summed = (
        lax.psum(shares[0].astype(jnp.bfloat16), "ctx").astype(jnp.float32),
        lax.psum(shares[1].astype(jnp.bfloat16), "ctx").astype(jnp.float32),
        lax.psum(shares[2].astype(jnp.bfloat16), "ctx").astype(jnp.float32),
        lax.psum(shares[3].astype(jnp.bfloat16), "ctx").astype(jnp.float32),
        lax.psum(shares[4].astype(jnp.bfloat16), "ctx").astype(jnp.float32),
        lax.psum(shares[5].astype(jnp.bfloat16), "ctx").astype(jnp.float32),
        lax.psum(shares[6].astype(jnp.bfloat16), "ctx").astype(jnp.float32),
        lax.psum(shares[7].astype(jnp.bfloat16), "ctx").astype(jnp.float32),
        lax.psum(shares[8].astype(jnp.bfloat16), "ctx").astype(jnp.float32),
        lax.psum(shares[9].astype(jnp.bfloat16), "ctx").astype(jnp.float32),
        lax.psum(shares[10].astype(jnp.bfloat16), "ctx").astype(jnp.float32),
        lax.psum(shares[11].astype(jnp.bfloat16), "ctx").astype(jnp.float32),
        lax.psum(shares[12].astype(jnp.bfloat16), "ctx").astype(jnp.float32),
        lax.psum(shares[13].astype(jnp.bfloat16), "ctx").astype(jnp.float32),
        lax.psum(shares[14].astype(jnp.bfloat16), "ctx").astype(jnp.float32),
    )
    return (
        output[None],
        input_grad[None],
        summed[0],
        summed[1],
        summed[2],
        summed[3],
        summed[4],
        summed[5],
        summed[6],
        summed[7],
        summed[8],
        summed[9],
        summed[10],
        summed[11],
        summed[12],
        summed[13],
        summed[14],
        grad_taps,
    )


def solution(mesh):
    return jax.shard_map(
        per_device,
        mesh=mesh,
        in_specs=(
            P("fsdp", "ctx", None),
            P("fsdp", "ctx", None),
            P("fsdp"),
            P("fsdp", None),
            P("fsdp", None),
            P("fsdp", None),
            P("fsdp", None),
            P("fsdp", None),
            P("fsdp", None),
            P("fsdp"),
            P("fsdp"),
            P("fsdp"),
            P("fsdp"),
            P("fsdp"),
            P("fsdp"),
            P("fsdp"),
            P("fsdp"),
            P("fsdp"),
            P(),
        ),
        out_specs=(
            P("fsdp", "ctx", None),
            P("fsdp", "ctx", None),
            P("fsdp", None),
            P("fsdp", None),
            P("fsdp", None),
            P("fsdp", None),
            P("fsdp", None),
            P("fsdp", None),
            P("fsdp"),
            P("fsdp"),
            P("fsdp"),
            P("fsdp"),
            P("fsdp"),
            P("fsdp"),
            P("fsdp"),
            P("fsdp"),
            P("fsdp"),
            P(),
        ),
        check_vma=False,
    )
```

profile of v0, /device:TPU:1, one launch (start us, length us, event | category | flops | bytes accessed | tf_op | source)
XLA Modules:
  0.0 1065.8 jit_solution(17845931276929191577)
XLA Ops:
  21.7 31.6 %all-reduce.19 = (bf16[768]{0:T(1024)(128)(2,1)S(1)}, bf16[768]{0:T(1024)(128)(2,1)S(1)}, bf16[768]{0:T(1024)(128)(2,1)S(1)}, bf16[768]{0:T(1024)(128)(2,1)S(1)}...) all-reduce(bf16[768]{0:T(1024)(128)(2,1)S(1)} %dynamic-update-slice, ...), channel_id=1, replica_groups=mesh['ctx'=4,'fsdp'=8] {'fsdp'}, use_global_device_ids=true, to_apply=%add | all-reduce | flops 5376 | bytes 21504
  56.3 39.3 %all-gather.12.cloned.1.call-done = bf16[768,768]{1,0:T(8,128)(2,1)} async-done(((bf16[96,768]{1,0:T(8,128)(2,1)}), bf16[768,768]{1,0:T(8,128)(2,1)}) %all-gather.12.cloned.1.call-update) | async-done | bytes 1179664 | tf_op jit(solution)/shard_map/all_gather | solution.py:103
  98.3 39.9 %all-gather.16.cloned.1.call-done = bf16[768,768]{1,0:T(8,128)(2,1)} async-done(((bf16[96,768]{1,0:T(8,128)(2,1)}), bf16[768,768]{1,0:T(8,128)(2,1)}) %all-gather.16.cloned.1.call-update) | async-done | bytes 1179664 | tf_op jit(solution)/shard_map/all_gather | solution.py:104
  147.5 3.8 collective-permute-start.1
  153.7 21.5 %all-gather = bf16[8,1,384]{2,1,0:T(2,128)(2,1)S(1)} all-gather(bf16[1,1,384]{2,1,0:T(2,128)(2,1)S(1)} %reshape.496), channel_id=1, replica_groups=mesh['ctx'=4,'fsdp'=8] {'fsdp'}, dimensions={0}, use_global_device_ids=true | all-gather | bytes 6912 | tf_op jit(solution)/shard_map/all_gather | solution.py:111
  177.0 8.0 collective-permute-start
  256.3 3.2 fusion.290
  264.4 9.2 fusion.30
  276.7 62.7 %all-gather.22.cloned.1.call-done = bf16[768,3072]{1,0:T(8,128)(2,1)} async-done(((bf16[96,3072]{1,0:T(8,128)(2,1)}), bf16[768,3072]{1,0:T(8,128)(2,1)}) %all-gather.22.cloned.1.call-update) | async-done | bytes 4718608 | tf_op jit(solution)/shard_map/all_gather | solution.py:106
  339.4 12.2 %multiply_convert_fusion.1 = (bf16[256,3072]{1,0:T(8,128)(2,1)}, f32[256,3072]{1,0:T(8,128)}, f32[256,3072]{1,0:T(8,128)}) fusion(f32[3072]{0:T(1024)} %bitcast.690, bf16[768,3072]{1,0:T(8,128)(2,1)} %all-gather.22.cloned.1.call-done, f32[256,768]{1,0:T(8,128)} %copy-done.4, f32[768]{0:T(1024)S(1)} %convert_element_type.696, ...), kind=kOutput, calls=%fused_computation.44 | convolution fusion | flops 1260847104 | bytes 13389824 | tf_op jit(solution)/shard_map/dot_general | solution.py:211
  351.7 67.7 %all-gather.24.cloned.1.call-done = bf16[3072,768]{1,0:T(8,128)(2,1)} async-done(((bf16[384,768]{1,0:T(8,128)(2,1)}), bf16[3072,768]{1,0:T(8,128)(2,1)}) %all-gather.24.cloned.1.call-update) | async-done | bytes 4718608 | tf_op jit(solution)/shard_map/all_gather | solution.py:107
  419.4 4.6 fusion.293
  426.5 2.8 fusion.277
  443.0 30.0 %all-reduce.31.cloned.1.call-done = (bf16[12,64,64]{2,1,0:T(8,128)(2,1)}, bf16[64,768]{1,0:T(8,128)(2,1)}) async-done(((bf16[12,64,64]{2,1,0:T(8,128)(2,1)}, bf16[64,768]{1,0:T(8,128)(2,1)}), (bf16[12,64,64]{2,1,0:T(8,128)(2,1)}, bf16[64,768]{1,0:T(8,128)(2,1)})) %all-reduce.31.cloned.1.call-update) | async-done | bytes 196624 | tf_op jit(solution)/shard_map/psum | solution.py:268
  529.0 3.9 collective-permute-start.3
  537.5 2.8 fusion.136
  563.3 3.2 fusion.124
  580.2 3.1 fusion.112
  597.1 3.3 fusion.154
  614.1 3.2 fusion.142
  632.0 10.9 %fusion.279 = (bf16[12,64]{1,0:T(8,128)(2,1)S(1)}, bf16[256,12,64]{0,2,1:T(8,128)(2,1)S(1)}, bf16[256,12,64]{0,2,1:T(8,128)(2,1)}) fusion(bf16[256]{0:T(256)(128)(2,1)S(1)} %copy-done.146, f32[256,12,64]{0,2,1:T(8,128)S(1)} %bitcast.583, f32[12]{0:T(128)S(1)} %copy-done.164, f32[256,12,64]{0,2,1:T(8,128)} %bitcast.584, f32[12]{0:T(128)S(1)} %copy-done.165, ...), kind=kOutput, calls=%fused_computation.550 | convolution fusion | flops 38927616 | bytes 26840628 | tf_op jit(solution)/shard_map/hit,hie->the/dot_general | solution.py:290
  646.8 4.3 convolution_convert_fusion.1
  652.6 3.6 convolution_convert_fusion
  658.2 4.6 fusion.87
  664.4 4.2 fusion.86
  671.9 40.0 %psum.159 = f32[12,33]{1,0:T(8,128)} all-reduce(f32[12,33]{1,0:T(8,128)S(1)} %stack.135), channel_id=1, replica_groups=mesh['ctx'=4,'fsdp'=8] {'ctx','fsdp'}, use_global_device_ids=true, to_apply=%region_67.68 | all-reduce | flops 396 | bytes 3168 | tf_op jit(solution)/shard_map/psum | solution.py:308
  715.4 11.9 %reduce-scatter.23.cloned.1.call-done = bf16[96,768]{1,0:T(8,128)(2,1)} async-done(((bf16[768,768]{1,0:T(8,128)(2,1)}), bf16[96,768]{1,0:T(8,128)(2,1)}) %reduce-scatter.23.cloned.1.call-update) | async-done | bytes 147472
  729.0 65.4 %reduce-scatter.13.cloned.1.call-done = bf16[96,768]{1,0:T(8,128)(2,1)} async-done(((bf16[768,768]{1,0:T(8,128)(2,1)}), bf16[96,768]{1,0:T(8,128)(2,1)}) %reduce-scatter.13.cloned.1.call-update) | async-done | bytes 147472 | tf_op jit(solution)/shard_map/reduce_scatter | solution.py:345
  794.4 100.2 %reduce-scatter.15.cloned.1.call-done = bf16[96,3072]{1,0:T(8,128)(2,1)} async-done(((bf16[768,3072]{1,0:T(8,128)(2,1)}), bf16[96,3072]{1,0:T(8,128)(2,1)}) %reduce-scatter.15.cloned.1.call-update) | async-done | bytes 589840 | tf_op jit(solution)/shard_map/reduce_scatter | solution.py:348
  894.5 98.8 %reduce-scatter.17.cloned.1.call-done = bf16[384,768]{1,0:T(8,128)(2,1)} async-done(((bf16[3072,768]{1,0:T(8,128)(2,1)}), bf16[384,768]{1,0:T(8,128)(2,1)}) %reduce-scatter.17.cloned.1.call-update) | async-done | bytes 589840 | tf_op jit(solution)/shard_map/reduce_scatter | solution.py:351
  995.3 29.1 %all-reduce.18 = (bf16[768]{0:T(1024)(128)(2,1)S(1)}, bf16[768]{0:T(1024)(128)(2,1)S(1)}, bf16[768]{0:T(1024)(128)(2,1)S(1)}, bf16[768]{0:T(1024)(128)(2,1)S(1)}...) all-reduce(bf16[768]{0:T(1024)(128)(2,1)S(1)} %dynamic-update-slice, ...), channel_id=1, replica_groups=mesh['ctx'=4,'fsdp'=8] {'fsdp'}, use_global_device_ids=true, to_apply=%add.7 | all-reduce | flops 9984 | bytes 39936
  1025.1 13.1 %all-reduce.20 = (bf16[96]{0:T(256)(128)(2,1)S(1)}, bf16[96]{0:T(256)(128)(2,1)S(1)}, bf16[96]{0:T(256)(128)(2,1)S(1)}, bf16[384]{0:T(512)(128)(2,1)S(1)}, bf16[...) all-reduce(bf16[96]{0:T(256)(128)(2,1)S(1)} %dynamic-slice.9, ...), channel_id=1, replica_groups=mesh['ctx'=4,'fsdp'=8] {'ctx'}, use_global_device_ids=true, to_apply=%region_42.43 | all-reduce | flops 1152 | bytes 4608 | tf_op jit(solution)/shard_map/psum | solution.py:389
  (829 shorter events, 302.9 us)
Async XLA Ops:
  7.2 46.3 %all-gather.10.cloned.1.call-start = ((), (), s32[]{:S(2)}) async-start(), calls=%async_computation.6 | async-start | bytes 1327104 | tf_op jit(solution)/shard_map/all_gather | solution.py:102
  9.0 86.7 %all-gather.12.cloned.1.call-start = ((), (), s32[]{:S(2)}) async-start(), calls=%async_computation.7 | async-start | bytes 1327104 | tf_op jit(solution)/shard_map/all_gather | solution.py:103
  10.7 127.6 %all-gather.16.cloned.1.call-start = ((), (), s32[]{:S(2)}) async-start(), calls=%async_computation.9 | async-start | bytes 1327104 | tf_op jit(solution)/shard_map/all_gather | solution.py:104
  12.4 211.4 %all-reduce.27.cloned.1.call-start = ((), (), s32[]{:S(2)}) async-start(), calls=%async_computation.20 | async-start | bytes 786432 | tf_op jit(solution)/shard_map/psum | solution.py:161
  98.3 152.8 %all-gather.18.cloned.1.call-start = ((), (), s32[]{:S(2)}) async-start(), calls=%async_computation.10 | async-start | bytes 1966080 | tf_op jit(solution)/shard_map/all_gather | solution.py:181
  140.8 112.9 %all-gather.14.cloned.1.call-start = ((), (), s32[]{:S(2)}) async-start(), calls=%async_computation.8 | async-start | bytes 1966080 | tf_op jit(solution)/shard_map/all_gather | solution.py:180
  141.4 132.2 %all-gather.20.cloned.1.call-start = ((), (), s32[]{:S(2)}) async-start(), calls=%async_computation.11 | async-start | bytes 1327104 | tf_op jit(solution)/shard_map/all_gather | solution.py:105
  142.1 197.3 %all-gather.22.cloned.1.call-start = ((), (), s32[]{:S(2)}) async-start(), calls=%async_computation.12 | async-start | bytes 5308416 | tf_op jit(solution)/shard_map/all_gather | solution.py:106
  143.1 276.2 %all-gather.24.cloned.1.call-start = ((), (), s32[]{:S(2)}) async-start(), calls=%async_computation.13 | async-start | bytes 5308416 | tf_op jit(solution)/shard_map/all_gather | solution.py:107
  145.3 327.6 %all-reduce.31.cloned.1.call-start = ((), (), s32[]{:S(2)}) async-start(), calls=%async_computation.22 | async-start | bytes 589824 | tf_op jit(solution)/shard_map/psum | solution.py:268
  147.5 37.4 %collective-permute-start.1 = (bf16[16,768]{1,0:T(8,128)(2,1)S(1)}, bf16[16,768]{1,0:T(8,128)(2,1)S(1)}, u32[]{:S(2)}, u32[]{:S(2)}) collective-permute-start(bf16[16,768]{1,0:T(8,128)(2,1)S(1)} %get-tuple-element.275), channel_id=1, source_target_pairs={{8,0},{16,8},{24,16},{9,1},{17,9},{25,17},{10,2},{18,10},{26,18},{... | collective-permute-start | bytes 73736 | tf_op jit(solution)/shard_map/ppermute | solution.py:30
  177.0 11.9 %collective-permute-start = (bf16[16,768]{1,0:T(8,128)(2,1)S(1)}, bf16[16,768]{1,0:T(8,128)(2,1)S(1)}, u32[]{:S(2)}, u32[]{:S(2)}) collective-permute-start(bf16[16,768]{1,0:T(8,128)(2,1)S(1)} %get-tuple-element.274), channel_id=1, source_target_pairs={{0,8},{8,16},{16,24},{1,9},{9,17},{17,25},{2,10},{10,18},{18,26},{... | collective-permute-start | bytes 73736 | tf_op jit(solution)/shard_map/ppermute | solution.py:27
  442.1 269.8 %reduce-scatter.21.cloned.1.call-start = ((), (), s32[]{:S(2)}) async-start(), calls=%async_computation.18 | async-start | bytes 1327104
  527.8 185.8 %reduce-scatter.19.cloned.1.call-start = ((), (), s32[]{:S(2)}) async-start(), calls=%async_computation.17 | async-start | bytes 1327104
  529.0 8.5 collective-permute-start.3
  534.1 12.8 %collective-permute-start.2 = (bf16[16,768]{1,0:T(8,128)(2,1)}, bf16[16,768]{1,0:T(8,128)(2,1)}, u32[]{:S(2)}, u32[]{:S(2)}) collective-permute-start(bf16[16,768]{1,0:T(8,128)(2,1)} %get-tuple-element.272), channel_id=1, source_target_pairs={{8,0},{16,8},{24,16},{9,1},{17,9},{25,17},{10,2},{18,10},{26,18},{... | collective-permute-start | bytes 73736 | tf_op jit(solution)/shard_map/ppermute | solution.py:30
  546.7 180.6 %reduce-scatter.23.cloned.1.call-start = ((), (), s32[]{:S(2)}) async-start(), calls=%async_computation.19 | async-start | bytes 1327104
  645.2 149.2 %reduce-scatter.13.cloned.1.call-start = ((), (), s32[]{:S(2)}) async-start(), calls=%async_computation.14 | async-start | bytes 1327104 | tf_op jit(solution)/shard_map/reduce_scatter | solution.py:345
  646.8 247.8 %reduce-scatter.15.cloned.1.call-start = ((), (), s32[]{:S(2)}) async-start(), calls=%async_computation.15 | async-start | bytes 5308416 | tf_op jit(solution)/shard_map/reduce_scatter | solution.py:348
  651.2 342.1 %reduce-scatter.17.cloned.1.call-start = ((), (), s32[]{:S(2)}) async-start(), calls=%async_computation.16 | async-start | bytes 5308416 | tf_op jit(solution)/shard_map/reduce_scatter | solution.py:351
  656.3 392.2 %all-reduce.29.cloned.1.call-start = ((), (), s32[]{:S(2)}) async-start(), calls=%async_computation.21 | async-start | bytes 3833856 | tf_op jit(solution)/shard_map/psum | solution.py:383
  668.7 324.7 %copy-start.27 = (f32[256,768]{1,0:T(8,128)S(1)}, f32[256,768]{1,0:T(8,128)}, u32[]{:S(2)}) copy-start(f32[256,768]{1,0:T(8,128)} %copy-done.26) | copy-start | bytes 2359300
  668.7 324.7 %copy-start.105 = (bf16[256,768]{1,0:T(8,128)(2,1)S(1)}, bf16[256,768]{1,0:T(8,128)(2,1)}, u32[]{:S(2)}) copy-start(bf16[256,768]{1,0:T(8,128)(2,1)} %copy-done.104) | copy-start | bytes 1179652
  668.7 324.7 %copy-start.129 = (f32[256]{0:T(256)S(1)}, f32[256]{0:T(256)}, u32[]{:S(2)}) copy-start(f32[256]{0:T(256)} %copy-done.128) | copy-start | bytes 3076
  671.7 323.6 %copy-start.130 = (bf16[768]{0:T(1024)(128)(2,1)S(1)}, bf16[768]{0:T(1024)(128)(2,1)}, u32[]{:S(2)}) copy-start(bf16[768]{0:T(1024)(128)(2,1)} %get-tuple-element.74) | copy-start | bytes 4612
  671.7 323.6 %copy-start.131 = (bf16[768]{0:T(1024)(128)(2,1)S(1)}, bf16[768]{0:T(1024)(128)(2,1)}, u32[]{:S(2)}) copy-start(bf16[768]{0:T(1024)(128)(2,1)} %get-tuple-element.79) | copy-start | bytes 4612
  671.7 323.6 %copy-start.132 = (bf16[768]{0:T(1024)(128)(2,1)S(1)}, bf16[768]{0:T(1024)(128)(2,1)}, u32[]{:S(2)}) copy-start(bf16[768]{0:T(1024)(128)(2,1)} %get-tuple-element.182) | copy-start | bytes 4612
  671.7 323.6 %copy-start.133 = (bf16[768]{0:T(1024)(128)(2,1)S(1)}, bf16[768]{0:T(1024)(128)(2,1)}, u32[]{:S(2)}) copy-start(bf16[768]{0:T(1024)(128)(2,1)} %get-tuple-element.186) | copy-start | bytes 4612
  671.7 323.6 %copy-start.148 = (bf16[3072]{0:T(1024)(128)(2,1)S(1)}, bf16[3072]{0:T(1024)(128)(2,1)}, u32[]{:S(2)}) copy-start(bf16[3072]{0:T(1024)(128)(2,1)} %get-tuple-element.184) | copy-start | bytes 18436
  671.7 323.6 %copy-start.199 = (bf16[768]{0:T(1024)(128)(2,1)S(1)}, bf16[768]{0:T(1024)(128)(2,1)}, u32[]{:S(2)}) copy-start(bf16[768]{0:T(1024)(128)(2,1)} %get-tuple-element.72) | copy-start | bytes 4612
  671.9 371.1 %copy-start.106 = (bf16[256,12,64]{0,2,1:T(8,128)(2,1)S(1)}, bf16[256,12,64]{0,2,1:T(8,128)(2,1)}, u32[]{:S(2)}) copy-start(bf16[256,12,64]{0,2,1:T(8,128)(2,1)} %get-tuple-element.304) | copy-start | bytes 1179652
  715.4 327.7 %copy-start.60 = (bf16[256,768]{1,0:T(8,128)(2,1)S(1)}, bf16[256,768]{1,0:T(8,128)(2,1)}, u32[]{:S(2)}) copy-start(bf16[256,768]{1,0:T(8,128)(2,1)} %copy-done.59) | copy-start | bytes 1179652
  (207 other events, 2945.5 us)
Sparse Core Ops, SparseCore 0:
  10.8 42.1 all-gather.9
  55.7 39.8 all-gather.11
  98.4 39.7 all-gather.15
  141.0 31.2 all-reduce.26
  173.7 21.5 all-gather.17
  197.4 19.6 all-gather.13
  219.8 39.5 all-gather.19
  261.6 77.8 all-gather.21
  341.6 77.6 all-gather.23
  442.2 30.6 all-reduce.30
  527.9 64.3 reduce-scatter.20
  596.1 63.7 reduce-scatter.18
  663.3 63.9 reduce-scatter.22
  730.5 63.8 reduce-scatter.12
  797.9 96.6 reduce-scatter.14
  898.0 95.2 reduce-scatter.16
  996.6 48.6 all-reduce.28
where the time goes:
time: 1070 us
  waiting for transfers between devices  517 us (48%)
  local copies, waits for them, and re-layouts  153 us (14%)
  matrix products  148 us (14%)
  blocking collectives  135 us (13%)
  other arithmetic  73.3 us (7%)
  between operations  20.8 us (2%)
  starting transfers between devices  19 us (2%)
    reduce_scatter x1, waiting for transfers between devices, per_device(): lax.psum_scatter(grad_up.astype(jnp.bfloat16), 'fsdp', scatter_dimension=...  100 us
    reduce_scatter x1, waiting for transfers between devices, per_device(): lax.psum_scatter(grad_down.astype(jnp.bfloat16), 'fsdp', scatter_dimensio...  98.8 us
    convert_element_type x32, local copies, waits for them, and re-layouts, conv_transpose(): taps[:, offset][None, :, None] * padded_heads[begin:begin + count]  68.8 us
    all_gather x1, waiting for transfers between devices, per_device(): lax.all_gather(w_down.astype(jnp.bfloat16), 'fsdp', axis=0, tiled=True)  67.7 us
    reduce_scatter x1, waiting for transfers between devices, per_device(): lax.psum_scatter(grad_out.astype(jnp.bfloat16), 'fsdp', scatter_dimension...  65.4 us
    all_gather x1, waiting for transfers between devices, per_device(): lax.all_gather(w_up.astype(jnp.bfloat16), 'fsdp', axis=0, tiled=True)  62.7 us
    unnamed x2, blocking collectives  60.7 us
    psum x1, blocking collectives, per_device(): grad_taps = lax.psum(taps_local, ('ctx', 'fsdp'))  40 us
  transfers between devices with their start and end apart: 21, of which 9 were waited for; matrix products, arithmetic and copies ran while one was open for 26% of the time, Pallas kernels for 0%

commit v1 on v0

v1 whole, which is shorter than its diff:
```python
import jax
import jax.numpy as jnp
from jax import lax
from jax.experimental import pallas as pl
from jax.experimental.pallas import tpu as pltpu
from jax.sharding import PartitionSpec as P

D = 768
HEADS = 12
HEAD_DIM = 64
FF = 3072
LAND = 64
KSIZE = 33
ITERS = 6
HALF = 16

F32 = jnp.float32
BF = jnp.bfloat16
highest = lax.Precision.HIGHEST
norm_eps = 1e-05
masked_score = -1e30
CONV_OUT = 256
CONV_IN = 512
TAPS_OUT = 128
TAPS_IN = 384


def nn(a, b, **kw):
    return lax.dot_general(a, b, (((1,), (0,)), ((), ())), preferred_element_type=F32, **kw)


def nt(a, b, **kw):
    return lax.dot_general(a, b, (((1,), (1,)), ((), ())), preferred_element_type=F32, **kw)


def tn(a, b, **kw):
    return lax.dot_general(a, b, (((0,), (0,)), ((), ())), preferred_element_type=F32, **kw)


def shape(dims, dtype):
    return jax.ShapeDtypeStruct(dims, dtype)


SMEM = pl.BlockSpec(memory_space=pltpu.SMEM)
VMEM = pl.BlockSpec(memory_space=pltpu.VMEM)
ANY = pl.BlockSpec(memory_space=pl.ANY)


def swap(block, axis, key):
    count = lax.axis_size(axis)
    return lax.ppermute(block, axis, [(i, i ^ key) for i in range(count)])


def iota(dims, axis):
    return lax.broadcasted_iota(jnp.int32, dims, axis)


def fetch(copies):
    for copy in copies:
        copy.start()
    for copy in copies:
        copy.wait()


def halves(value):
    high = value.astype(BF)
    low = (value - high.astype(F32)).astype(BF)
    return high, low


def taps_kernel(base_ref, ahead_ref, back_ref):
    heads = base_ref.shape[0]
    for head in range(heads):
        for row, out_ref in ((0, ahead_ref), (1, back_ref)):
            line = jnp.broadcast_to(base_ref[head, row : row + 1, :], (CONV_IN, CONV_IN))
            band = pltpu.roll(line, 0, 1, stride=1, stride_axis=0)[:, :CONV_OUT]
            high, low = halves(band)
            out_ref[head, 0] = high
            out_ref[head, 1] = low


def taps_bands(taps):
    heads = taps.shape[0]
    ahead = jnp.pad(taps[:, ::-1], ((0, 0), (CONV_IN - 144, 144 - KSIZE)))
    back = jnp.pad(taps, ((0, 0), (CONV_IN - 144, 144 - KSIZE)))
    base = jnp.stack([ahead, back], axis=1)
    base = jnp.pad(base, ((0, 0), (0, 6), (0, 0)))
    band = shape((heads, 2, CONV_IN, CONV_OUT), BF)
    return pl.pallas_call(taps_kernel, out_shape=(band, band), name="bands")(base)


def conv_band(line, band_ref, head):
    slots = line.shape[1]
    blocks = slots // CONV_OUT
    edge = jnp.zeros((line.shape[0], 128), line.dtype)
    padded = jnp.concatenate([edge, line, edge], axis=1)
    stacked = jnp.concatenate(
        [padded[:, CONV_OUT * b : CONV_OUT * b + CONV_IN] for b in range(blocks)], axis=0
    )
    product = nn(stacked, band_ref[head, 0]) + nn(stacked, band_ref[head, 1])
    rows = line.shape[0]
    return jnp.concatenate([product[rows * b : rows * (b + 1)] for b in range(blocks)], axis=1)


def softmax_rows(scores):
    top = jnp.max(scores, axis=1, keepdims=True)
    powers = jnp.exp(scores - top)
    return powers / jnp.sum(powers, axis=1, keepdims=True)


def softmax_columns(scores):
    top = jnp.max(scores, axis=0, keepdims=True)
    powers = jnp.exp(scores - top)
    return powers / jnp.sum(powers, axis=0, keepdims=True)


def segments(slots, length):
    spot = iota((LAND, slots), 1)
    scaled = spot * LAND
    mark = iota((LAND, slots), 0) * length
    inside = (scaled >= mark) & (scaled < mark + length) & (spot < length)
    return jnp.where(inside, 1.0, 0.0)


def attend_kernel(parts, count_ctx, count_fsdp, *refs):
    heads, rows, shard = parts
    width = heads * HEAD_DIM
    refs = list(refs)
    scalar_ref = refs.pop(0)
    token_refs = [refs.pop(0) for _ in range(count_ctx)]
    weight_refs = [refs.pop(0) for _ in range(count_fsdp)]
    band_ref = refs.pop(0)
    (
        seq_ref,
        turned_ref,
        qkv_ref,
        small_ref,
        land_ref,
        state_ref,
        blocks_ref,
        joined_ref,
        extra_ref,
        mixed_ref,
        copy_sem,
    ) = refs
    own_ctx = scalar_ref[0]
    own_fsdp = scalar_ref[1]
    length = scalar_ref[2]
    slots = rows * count_ctx
    copies = []
    for key in range(count_ctx):
        spot = pl.multiple_of(jnp.bitwise_xor(own_ctx, key) * rows, rows)
        copies.append(
            pltpu.make_async_copy(
                token_refs[key], seq_ref.at[pl.ds(spot, rows), :], copy_sem.at[len(copies)]
            )
        )
    for key in range(count_fsdp):
        owner = jnp.bitwise_xor(own_fsdp, key)
        spot = pl.multiple_of(owner * shard, 8)
        copies.append(
            pltpu.make_async_copy(
                weight_refs[key].at[pl.ds(0, shard), :],
                joined_ref.at[pl.ds(spot, shard), :],
                copy_sem.at[len(copies)],
            )
        )
        spot = pl.multiple_of(owner * 8, 8)
        copies.append(
            pltpu.make_async_copy(
                weight_refs[key].at[pl.ds(shard, 8), :],
                extra_ref.at[pl.ds(spot, 8), :],
                copy_sem.at[len(copies)],
            )
        )
    fetch(copies)
    small_ref[...] = extra_ref[...]
    turned_ref[...] = joined_ref[...].T

    entry = iota((3 * width, 1), 0)
    kind = jnp.where(entry >= 2 * width, 2, jnp.where(entry >= width, 1, 0))
    spot = own_ctx * width + entry - kind * width
    owner = jnp.floor((spot.astype(F32) + 0.5) * (1.0 / shard)).astype(jnp.int32)
    lane = spot - owner * shard
    source = owner * 8 + jnp.where(kind == 2, 1, 0)
    wanted = (kind != 1) & (spot < D)
    choice = (iota((3 * width, count_fsdp * 8), 1) == source) & wanted
    spread = nn(choice.astype(BF), extra_ref[:, :128])
    bias = jnp.sum(
        jnp.where(iota((3 * width, 128), 1) == lane, spread, 0.0), axis=1, keepdims=True
    )
    scale = jnp.where(kind == 0, 0.125, 1.0)

    for chunk in range(slots // 256):
        begin = chunk * 256
        product = nt(turned_ref[...], seq_ref[begin : begin + 256, :])
        live = (iota((1, 256), 1) + begin) < length
        qkv_ref[:, begin : begin + 256] = jnp.where(live, (product + bias) * scale, 0.0).astype(BF)

    table = segments(slots, length)
    counts = jnp.sum(table, axis=1, keepdims=True)
    table_low = table.astype(BF)
    live = iota((1, slots), 1) < length

    def gather_head(head, carry):
        q = qkv_ref[pl.ds(pl.multiple_of(head * HEAD_DIM, HEAD_DIM), HEAD_DIM), :]
        k = qkv_ref[pl.ds(pl.multiple_of(width + head * HEAD_DIM, HEAD_DIM), HEAD_DIM), :]
        v = qkv_ref[pl.ds(pl.multiple_of(2 * width + head * HEAD_DIM, HEAD_DIM), HEAD_DIM), :]
        land_query = nt(table_low, q) / counts
        land_keys = nt(table_low, k) / counts
        land_ref[0, head] = land_query
        land_ref[1, head] = land_keys
        scores = nn(land_query.astype(BF), k)
        weights = softmax_rows(jnp.where(live, scores, masked_score))
        land_ref[2, head] = nt(weights.astype(BF), v)
        return carry

    lax.fori_loop(0, heads, gather_head, 0)

    every = range(heads)
    eye = (iota((LAND, LAND), 0) == iota((LAND, LAND), 1)).astype(F32)
    kernels = [softmax_rows(nt(land_ref[0, h], land_ref[1, h], precision=highest)) for h in every]
    starts = []
    for h in every:
        land_ref[4, h] = kernels[h]
        column_top = jnp.max(jnp.sum(kernels[h], axis=0, keepdims=True), axis=1, keepdims=True)
        row_top = jnp.max(jnp.sum(kernels[h], axis=1, keepdims=True), axis=0, keepdims=True)
        starts.append(kernels[h].T / (column_top * row_top))

    def refine(step, approx):
        product = [nn(kernels[h], approx[h], precision=highest) for h in every]
        second = [15.0 * eye - nn(product[h], 7.0 * eye - product[h], precision=highest) for h in every]
        third = [13.0 * eye - nn(product[h], second[h], precision=highest) for h in every]
        for h in every:
            state_ref[step, 0, h] = approx[h]
            state_ref[step, 1, h] = product[h]
            state_ref[step, 2, h] = second[h]
            state_ref[step, 3, h] = third[h]
        return [0.25 * nn(approx[h], third[h], precision=highest) for h in every]

    inverse = lax.fori_loop(0, ITERS, refine, starts)
    for h in every:
        land_ref[3, h] = inverse[h]
        land_ref[5, h] = nn(inverse[h], land_ref[2, h], precision=highest)

    def mix_head(head, carry):
        q = qkv_ref[pl.ds(pl.multiple_of(head * HEAD_DIM, HEAD_DIM), HEAD_DIM), :]
        v = qkv_ref[pl.ds(pl.multiple_of(2 * width + head * HEAD_DIM, HEAD_DIM), HEAD_DIM), :]
        weights = softmax_columns(nn(land_ref[1, head].astype(BF), q))
        turned = land_ref[5, head].T.astype(BF)
        total = nn(turned, weights.astype(BF)) + conv_band(v, band_ref, head)
        mixed_ref[pl.ds(pl.multiple_of(head * HEAD_DIM, HEAD_DIM), HEAD_DIM), :] = total.astype(BF)
        return carry

    lax.fori_loop(0, heads, mix_head, 0)
    for key in range(count_ctx):
        spot = pl.multiple_of(jnp.bitwise_xor(own_ctx, key) * rows, rows)
        blocks_ref[key] = mixed_ref[:, pl.ds(spot, rows)]


def attend(scalars, tokens, weights, bands, heads, rows, shard):
    count_ctx, count_fsdp = len(tokens), len(weights)
    width = heads * HEAD_DIM
    slots = rows * count_ctx
    outs = (
        shape((slots, D), BF),
        shape((3 * width, D), BF),
        shape((3 * width, slots), BF),
        shape((count_fsdp * 8, 3 * width), BF),
        shape((6, heads, LAND, LAND), F32),
        shape((ITERS, 4, heads, LAND, LAND), F32),
        shape((count_ctx, width, rows), BF),
    )

    def body(*refs):
        attend_kernel((heads, rows, shard), count_ctx, count_fsdp, *refs)

    return pl.pallas_call(
        body,
        out_shape=outs,
        in_specs=[SMEM] + [ANY] * (count_ctx + count_fsdp) + [VMEM],
        out_specs=[VMEM] * len(outs),
        scratch_shapes=[
            pltpu.VMEM((D, 3 * width), BF),
            pltpu.VMEM((count_fsdp * 8, 3 * width), BF),
            pltpu.VMEM((width, slots), BF),
            pltpu.SemaphoreType.DMA((count_ctx + 2 * count_fsdp,)),
        ],
        cost_estimate=pl.CostEstimate(
            flops=4 * slots * D * 3 * width, bytes_accessed=60_000_000, transcendentals=0
        ),
        name="attend",
    )(scalars, *tokens, *weights, bands)


def attend_back_kernel(parts, count_ctx, count_fsdp, *refs):
    heads, rows, shard = parts
    width = heads * HEAD_DIM
    refs = list(refs)
    scalar_ref = refs.pop(0)
    grad_refs = [refs.pop(0) for _ in range(count_ctx)]
    (
        seq_ref,
        turned_ref,
        qkv_ref,
        land_ref,
        state_ref,
        band_ref,
        share_ref,
        keep_ref,
        send_ref,
        grad_ref,
        deep_ref,
        back_ref,
        taps_ref,
        copy_sem,
    ) = refs
    own_ctx = scalar_ref[0]
    length = scalar_ref[2]
    slots = rows * count_ctx
    copies = []
    for key in range(count_ctx):
        spot = pl.multiple_of(jnp.bitwise_xor(own_ctx, key) * rows, rows)
        copies.append(
            pltpu.make_async_copy(
                grad_refs[key], grad_ref.at[:, pl.ds(spot, rows)], copy_sem.at[key]
            )
        )
    fetch(copies)
    table = segments(slots, length)
    counts = jnp.sum(table, axis=1, keepdims=True)
    table_low = table.astype(BF)
    live = iota((1, slots), 1) < length
    every = range(heads)

    def rows_of(base, head):
        return pl.ds(pl.multiple_of(base + head * HEAD_DIM, HEAD_DIM), HEAD_DIM)

    def first(head, carry):
        q = qkv_ref[rows_of(0, head), :]
        g = grad_ref[rows_of(0, head), :]
        keys_low = land_ref[1, head].astype(BF)
        weights = softmax_columns(nn(keys_low, q))
        grad_mixing = nt(weights.astype(BF), g)
        slope = nn(land_ref[5, head].astype(BF), g)
        slope = (weights * (slope - jnp.sum(weights * slope, axis=0, keepdims=True))).astype(BF)
        deep_ref[1, head] = grad_mixing
        deep_ref[3, head] = nt(slope, q)
        back_ref[rows_of(0, head), :] = tn(keys_low, slope)
        return carry

    lax.fori_loop(0, heads, first, 0)
    for h in every:
        deep_ref[0, h] = nt(deep_ref[1, h], land_ref[2, h], precision=highest)
        deep_ref[1, h] = tn(land_ref[3, h], deep_ref[1, h], precision=highest)

    kernels = [land_ref[4, h] for h in every]
    eye = (iota((LAND, LAND), 0) == iota((LAND, LAND), 1)).astype(F32)

    def unwind(turn, carry):
        d_next, d_kernel = carry
        step = ITERS - 1 - turn
        approx = [state_ref[step, 0, h] for h in every]
        product = [state_ref[step, 1, h] for h in every]
        second = [state_ref[step, 2, h] for h in every]
        third = [state_ref[step, 3, h] for h in every]
        d_third = [0.25 * tn(approx[h], d_next[h], precision=highest) for h in every]
        d_approx = [0.25 * nt(d_next[h], third[h], precision=highest) for h in every]
        d_second = [-tn(product[h], d_third[h], precision=highest) for h in every]
        d_product = [-nt(d_third[h], second[h], precision=highest) for h in every]
        d_first = [-tn(product[h], d_second[h], precision=highest) for h in every]
        d_product = [
            d_product[h] - nt(d_second[h], 7.0 * eye - product[h], precision=highest) - d_first[h]
            for h in every
        ]
        d_kernel = [d_kernel[h] + nt(d_product[h], approx[h], precision=highest) for h in every]
        d_approx = [d_approx[h] + tn(kernels[h], d_product[h], precision=highest) for h in every]
        return d_approx, d_kernel

    d_start, d_kernel = lax.fori_loop(
        0,
        ITERS,
        unwind,
        ([deep_ref[0, h] for h in every], [jnp.zeros((LAND, LAND), F32) for _ in every]),
    )
    for h in every:
        kernel = kernels[h]
        column_sums = jnp.sum(kernel, axis=0, keepdims=True)
        row_sums = jnp.sum(kernel, axis=1, keepdims=True)
        column_top = jnp.max(column_sums, axis=1, keepdims=True)
        row_top = jnp.max(row_sums, axis=0, keepdims=True)
        scale = column_top * row_top
        turned = d_start[h].T
        d_scale = -jnp.sum(
            jnp.sum(turned * kernel, axis=1, keepdims=True), axis=0, keepdims=True
        ) / (scale * scale)
        column_hit = (column_sums == column_top).astype(F32)
        row_hit = (row_sums == row_top).astype(F32)
        column_hit = column_hit / jnp.sum(column_hit, axis=1, keepdims=True)
        row_hit = row_hit / jnp.sum(row_hit, axis=0, keepdims=True)
        slope = d_kernel[h] + turned / scale
        slope = slope + d_scale * row_top * column_hit + d_scale * column_top * row_hit
        slope = kernel * (slope - jnp.sum(kernel * slope, axis=1, keepdims=True))
        deep_ref[2, h] = nn(slope, land_ref[1, h], precision=highest)
        deep_ref[3, h] = deep_ref[3, h] + tn(slope, land_ref[0, h], precision=highest)

    table_twice = jnp.concatenate([table_low, table_low], axis=0)
    place, other = iota((TAPS_OUT, TAPS_OUT), 0), iota((TAPS_OUT, TAPS_OUT), 1)
    flip = (place + other == TAPS_OUT - 1).astype(BF)

    def second_pass(head, carry):
        k = qkv_ref[rows_of(width, head), :]
        v = qkv_ref[rows_of(2 * width, head), :]
        g = grad_ref[rows_of(0, head), :]
        query_low = land_ref[0, head].astype(BF)
        scores = nn(query_low, k)
        weights = softmax_rows(jnp.where(live, scores, masked_score))
        d_context = deep_ref[1, head].astype(BF)
        slope = nn(d_context, v)
        slope = (weights * (slope - jnp.sum(weights * slope, axis=1, keepdims=True))).astype(BF)
        d_query = (deep_ref[2, head] + nt(slope, k)) / counts
        d_keys = deep_ref[3, head] / counts
        high, low = halves(d_query)
        spread = tn(jnp.concatenate([high, low], axis=0), table_twice)
        d_q = (back_ref[rows_of(0, head), :] + spread).astype(BF)
        high, low = halves(d_keys)
        spread = tn(jnp.concatenate([high, low], axis=0), table_twice)
        d_k = (tn(query_low, slope) + spread).astype(BF)
        d_v = (tn(d_context, weights.astype(BF)) + conv_band(g, band_ref, head)).astype(BF)
        zero = jnp.zeros_like(d_q)
        back_ref[rows_of(0, head), :] = jnp.where(live, d_q.astype(F32) * 0.125, 0.0)
        back_ref[rows_of(width, head), :] = jnp.where(live, d_k.astype(F32), 0.0)
        back_ref[rows_of(2 * width, head), :] = jnp.where(live, d_v.astype(F32), 0.0)
        blocks = slots // TAPS_OUT
        edge = jnp.zeros((HEAD_DIM, TAPS_OUT), BF)
        padded = jnp.concatenate([edge, v, edge], axis=1)
        windows = jnp.concatenate(
            [padded[:, TAPS_OUT * b : TAPS_OUT * b + TAPS_IN] for b in range(blocks)], axis=0
        )
        places = jnp.concatenate(
            [g[:, TAPS_OUT * b : TAPS_OUT * (b + 1)] for b in range(blocks)], axis=0
        )
        flipped = nn(places, flip).astype(BF)
        square = tn(flipped, windows)
        slanted = pltpu.roll(square, TAPS_IN - 111 - TAPS_OUT, 1, stride=1, stride_axis=0)
        line = jnp.sum(slanted, axis=0, keepdims=True)
        taps_ref[pl.ds(pl.multiple_of(head * 8, 8), 8), :] = jnp.broadcast_to(
            line[:, :128], (8, 128)
        )
        return carry

    lax.fori_loop(0, heads, second_pass, 0)

    back_low = back_ref[...].astype(BF)
    entry = iota((width, 1), 0)
    spot = own_ctx * width + entry
    owner = jnp.floor((spot.astype(F32) + 0.5) * (1.0 / shard)).astype(jnp.int32)
    lane = spot - owner * shard
    pick_owner = ((iota((width, count_fsdp), 1) == owner) & (spot < D)).astype(F32)
    lines = []
    for base in (0, 2 * width):
        total = jnp.sum(back_ref[base : base + width, :], axis=1, keepdims=True)
        placed = jnp.where(iota((width, 128), 1) == lane, total, 0.0)
        lines.append(tn(pick_owner, placed, precision=highest))
    taps = jnp.concatenate(
        [taps_ref[8 * h : 8 * h + 1, :] for h in every]
        + [jnp.zeros((6 - heads, 128), F32)],
        axis=0,
    )
    taps = jnp.where(iota((6, 128), 1) < KSIZE, taps, 0.0)
    filler = jnp.zeros((8, 3 * width - 128), F32)
    grads = nn(back_low, seq_ref[...]).astype(BF).T
    for owner_index in range(count_fsdp):
        rest = jnp.concatenate(
            [lines[0][owner_index : owner_index + 1], lines[1][owner_index : owner_index + 1], taps],
            axis=0,
        )
        share_ref[owner_index, :shard] = grads[owner_index * shard : (owner_index + 1) * shard]
        share_ref[owner_index, shard:] = jnp.concatenate([rest, filler], axis=1).astype(BF)
    for key in range(count_ctx):
        spot = pl.multiple_of(jnp.bitwise_xor(own_ctx, key) * rows, rows)
        block = back_ref[:, pl.ds(spot, rows)].astype(BF)
        product = tn(block, turned_ref[...])
        if key % 2 == 0:
            keep_ref[key // 2] = product
        else:
            send_ref[key // 2] = product


def attend_back(scalars, grads, saved, bands, heads, rows, shard, count_fsdp):
    count_ctx = len(grads)
    width = heads * HEAD_DIM
    slots = rows * count_ctx
    sequence, turned, qkv, land, state = saved
    outs = (
        shape((count_fsdp, shard + 8, 3 * width), BF),
        shape((count_ctx // 2, rows, D), F32),
        shape((count_ctx // 2, rows, D), F32),
    )

    def body(*refs):
        attend_back_kernel((heads, rows, shard), count_ctx, count_fsdp, *refs)

    return pl.pallas_call(
        body,
        out_shape=outs,
        in_specs=[SMEM] + [ANY] * count_ctx + [VMEM] * 6,
        out_specs=[VMEM] * len(outs),
        scratch_shapes=[
            pltpu.VMEM((width, slots), BF),
            pltpu.VMEM((4, heads, LAND, LAND), F32),
            pltpu.VMEM((3 * width, slots), F32),
            pltpu.VMEM((8 * heads, 128), F32),
            pltpu.SemaphoreType.DMA((count_ctx,)),
        ],
        cost_estimate=pl.CostEstimate(
            flops=8 * slots * D * 3 * width, bytes_accessed=100_000_000, transcendentals=0
        ),
        name="attend_back",
    )(scalars, *grads, sequence, turned, qkv, land, state, bands)


def project_kernel(parts, count_ctx, count_fsdp, column, *refs):
    width, rows, shard = parts
    refs = list(refs)
    scalar_ref = refs.pop(0)
    mixed_refs = [refs.pop(0) for _ in range(count_ctx)]
    weight_refs = [refs.pop(0) for _ in range(count_fsdp)]
    (
        token_ref,
        small_ref,
        mixed_ref,
        out_ref,
        hidden_ref,
        low_ref,
        unit_ref,
        rate_ref,
        copy_sem,
    ) = refs
    own_ctx = scalar_ref[0]
    own_fsdp = scalar_ref[1]
    copies = []
    for key in range(count_ctx):
        spot = pl.multiple_of(jnp.bitwise_xor(own_ctx, key) * width, 8)
        copies.append(
            pltpu.make_async_copy(
                mixed_refs[key], mixed_ref.at[pl.ds(spot, width), :], copy_sem.at[len(copies)]
            )
        )
    for key in range(count_fsdp):
        spot = pl.multiple_of(jnp.bitwise_xor(own_fsdp, key) * shard, 8)
        copies.append(
            pltpu.make_async_copy(
                weight_refs[key].at[:, pl.ds(column, D)],
                out_ref.at[pl.ds(spot, shard), :],
                copy_sem.at[len(copies)],
            )
        )
    fetch(copies)
    mixer = tn(mixed_ref[:D, :], out_ref[...]) + small_ref[2:3, :]
    hidden_ref[...] = token_ref[...].astype(F32) + mixer

    def norm(step, carry):
        place = pl.ds(pl.multiple_of(step * 64, 64), 64)
        value = hidden_ref[place, :]
        average = jnp.mean(value, axis=-1, keepdims=True)
        centered = value - average
        rate = lax.rsqrt(jnp.mean(centered * centered, axis=-1, keepdims=True) + norm_eps)
        unit = centered * rate
        hidden = unit * small_ref[4:5, :] + small_ref[5:6, :]
        unit_ref[place, :] = unit
        rate_ref[place, :] = jnp.broadcast_to(rate, (64, 128))
        hidden_ref[place, :] = hidden
        low_ref[place, :] = hidden.astype(BF)
        return carry

    lax.fori_loop(0, rows // 64, norm, 0)


def project(scalars, mixed, weights, tokens, small, width, shard, column):
    count_ctx, count_fsdp = len(mixed), len(weights)
    rows = tokens.shape[0]
    outs = (
        shape((width * count_ctx, rows), BF),
        shape((D, D), BF),
        shape((rows, D), F32),
        shape((rows, D), BF),
        shape((rows, D), F32),
        shape((rows, 128), F32),
    )

    def body(*refs):
        project_kernel((width, rows, shard), count_ctx, count_fsdp, column, *refs)

    return pl.pallas_call(
        body,
        out_shape=outs,
        in_specs=[SMEM] + [ANY] * (count_ctx + count_fsdp) + [VMEM] * 2,
        out_specs=[VMEM] * len(outs),
        scratch_shapes=[pltpu.SemaphoreType.DMA((count_ctx + count_fsdp,))],
        cost_estimate=pl.CostEstimate(
            flops=2 * rows * D * D, bytes_accessed=12_000_000, transcendentals=0
        ),
        name="project",
    )(scalars, *mixed, *weights, tokens, small)


def lift_kernel(parts, count_fsdp, *refs):
    rows, shard, share = parts
    refs = list(refs)
    scalar_ref = refs.pop(0)
    own_ref = refs.pop(0)
    other_ref = refs.pop(0)
    up_refs = [refs.pop(0) for _ in range(count_fsdp)]
    down_refs = [refs.pop(0) for _ in range(count_fsdp)]
    (
        bias_ref,
        both_ref,
        up_ref,
        down_ref,
        active_ref,
        slope_ref,
        feed_ref,
        copy_sem,
    ) = refs
    own_fsdp = scalar_ref[1]
    copies = []
    for key in range(count_fsdp):
        owner = jnp.bitwise_xor(own_fsdp, key)
        spot = pl.multiple_of(owner * shard, 8)
        copies.append(
            pltpu.make_async_copy(
                up_refs[key].at[:, pl.ds(0, FF // 2)],
                up_ref.at[pl.ds(spot, shard), :],
                copy_sem.at[len(copies)],
            )
        )
        spot = pl.multiple_of(owner * share, 8)
        copies.append(
            pltpu.make_async_copy(
                down_refs[key], down_ref.at[pl.ds(spot, share), :], copy_sem.at[len(copies)]
            )
        )
    for copy in copies:
        copy.start()
    both_ref[:rows, :] = own_ref[...]
    both_ref[rows:, :] = other_ref[...]
    for copy in copies:
        copy.wait()

    def step(index, carry):
        place = pl.ds(pl.multiple_of(index * 128, 128), 128)
        lifted = nn(both_ref[place, :], up_ref[...]) + bias_ref[0:1, :]
        cdf = 0.5 * (1.0 + lax.erf(lifted * 0.7071067811865476))
        active = (lifted * cdf).astype(BF)
        active_ref[place, :] = active
        slope_ref[place, :] = cdf + lifted * (
            jnp.exp(-0.5 * lifted * lifted) * 0.3989422804014327
        )
        feed_ref[place, :] = nn(active, down_ref[...])
        return carry

    lax.fori_loop(0, 2 * rows // 128, step, 0)


def lift(scalars, own, other, ups, downs, bias, shard, share):
    count_fsdp = len(ups)
    rows = own.shape[0]
    outs = (
        shape((2 * rows, D), BF),
        shape((D, FF // 2), BF),
        shape((FF // 2, D), BF),
        shape((2 * rows, FF // 2), BF),
        shape((2 * rows, FF // 2), F32),
        shape((2 * rows, D), F32),
    )

    def body(*refs):
        lift_kernel((rows, shard, share), count_fsdp, *refs)

    return pl.pallas_call(
        body,
        out_shape=outs,
        in_specs=[SMEM, VMEM, VMEM] + [ANY] * (2 * count_fsdp) + [VMEM],
        out_specs=[VMEM] * len(outs),
        scratch_shapes=[pltpu.SemaphoreType.DMA((2 * count_fsdp,))],
        cost_estimate=pl.CostEstimate(
            flops=8 * rows * D * FF, bytes_accessed=40_000_000, transcendentals=0
        ),
        name="lift",
    )(scalars, own, other, *ups, *downs, bias)


def finish_kernel(
    scalar_ref,
    hidden_ref,
    own_ref,
    other_ref,
    small_ref,
    grad_ref,
    output_ref,
    second_ref,
    feed_ref,
    sums_ref,
):
    rows = hidden_ref.shape[0]
    begin = scalar_ref[0] * rows
    length = scalar_ref[2]

    def step(index, carry):
        gain_sum, shift_sum, feed_sum = carry
        place = pl.ds(pl.multiple_of(index * 64, 64), 64)
        value = hidden_ref[place, :] + (own_ref[place, :] + other_ref[place, :] + small_ref[3:4, :])
        average = jnp.mean(value, axis=-1, keepdims=True)
        centered = value - average
        rate = lax.rsqrt(jnp.mean(centered * centered, axis=-1, keepdims=True) + norm_eps)
        unit = centered * rate
        live = (iota((64, 1), 0) + begin + index * 64) < length
        normed = unit * small_ref[6:7, :] + small_ref[7:8, :]
        output_ref[place, :] = jnp.where(live, normed, 0.0).astype(BF)
        upstream = jnp.where(live, grad_ref[place, :].astype(F32), 0.0)
        scaled = upstream * small_ref[6:7, :]
        second = rate * (
            scaled
            - jnp.mean(scaled, axis=-1, keepdims=True)
            - unit * jnp.mean(scaled * unit, axis=-1, keepdims=True)
        )
        second_ref[place, :] = second
        low = second.astype(BF)
        feed_ref[place, :] = low

        def fold(block):
            return jnp.sum(block.reshape(8, 8, D), axis=0)

        return (
            gain_sum + fold(upstream * unit),
            shift_sum + fold(upstream),
            feed_sum + fold(low.astype(F32)),
        )

    zero = jnp.zeros((8, D), F32)
    totals = lax.fori_loop(0, rows // 64, step, (zero, zero, zero))
    sums_ref[...] = jnp.concatenate(
        [jnp.sum(total, axis=0, keepdims=True) for total in totals] + [jnp.zeros((5, D), F32)],
        axis=0,
    )


def finish(scalars, hidden, own, other, small, grads):
    rows = hidden.shape[0]
    outs = (
        shape((rows, D), BF),
        shape((rows, D), F32),
        shape((rows, D), BF),
        shape((8, D), F32),
    )
    return pl.pallas_call(
        finish_kernel,
        out_shape=outs,
        in_specs=[SMEM] + [VMEM] * 5,
        out_specs=[VMEM] * 4,
        cost_estimate=pl.CostEstimate(
            flops=30 * rows * D, bytes_accessed=9_000_000, transcendentals=0
        ),
        name="finish",
    )(scalars, hidden, own, other, small, grads)


def lower_kernel(
    own_ref, other_ref, slope_ref, up_ref, down_ref, both_ref, lifted_ref, hidden_ref, bias_ref
):
    rows = own_ref.shape[0]
    both_ref[:rows, :] = own_ref[...]
    both_ref[rows:, :] = other_ref[...]

    def step(index, total):
        place = pl.ds(pl.multiple_of(index * 128, 128), 128)
        slope = nt(both_ref[place, :], down_ref[...]) * slope_ref[place, :]
        low = slope.astype(BF)
        lifted_ref[place, :] = low
        hidden_ref[place, :] = nt(low, up_ref[...])
        return total + jnp.sum(low.astype(F32).reshape(16, 8, FF // 2), axis=0)

    total = lax.fori_loop(0, 2 * rows // 128, step, jnp.zeros((8, FF // 2), F32))
    bias_ref[...] = jnp.broadcast_to(jnp.sum(total, axis=0, keepdims=True), (8, FF // 2))


def lower(own, other, slope, up, down):
    rows = own.shape[0]
    outs = (
        shape((2 * rows, D), BF),
        shape((2 * rows, FF // 2), BF),
        shape((2 * rows, D), F32),
        shape((8, FF // 2), F32),
    )
    return pl.pallas_call(
        lower_kernel,
        out_shape=outs,
        in_specs=[VMEM] * 5,
        out_specs=[VMEM] * 4,
        cost_estimate=pl.CostEstimate(
            flops=8 * rows * D * FF, bytes_accessed=30_000_000, transcendentals=0
        ),
        name="lower",
    )(own, other, slope, up, down)


def unmix_kernel(
    parts,
    scalar_ref,
    second_ref,
    own_ref,
    other_ref,
    unit_ref,
    rate_ref,
    small_ref,
    weight_ref,
    first_ref,
    mixer_ref,
    blocks_ref,
    sums_ref,
    mixed_ref,
):
    width, count_ctx = parts
    rows = second_ref.shape[0]

    def step(index, carry):
        gain_sum, shift_sum, out_sum = carry
        place = pl.ds(pl.multiple_of(index * 64, 64), 64)
        upstream = (own_ref[place, :] + other_ref[place, :]) + second_ref[place, :]
        unit = unit_ref[place, :]
        scaled = upstream * small_ref[4:5, :]
        first = rate_ref[place, :1] * (
            scaled
            - jnp.mean(scaled, axis=-1, keepdims=True)
            - unit * jnp.mean(scaled * unit, axis=-1, keepdims=True)
        )
        first_ref[place, :] = first
        low = first.astype(BF)
        mixer_ref[place, :] = low

        def fold(block):
            return jnp.sum(block.reshape(8, 8, D), axis=0)

        return (
            gain_sum + fold(upstream * unit),
            shift_sum + fold(upstream),
            out_sum + fold(low.astype(F32)),
        )

    zero = jnp.zeros((8, D), F32)
    totals = lax.fori_loop(0, rows // 64, step, (zero, zero, zero))
    sums_ref[...] = jnp.concatenate(
        [jnp.sum(total, axis=0, keepdims=True) for total in totals] + [jnp.zeros((5, D), F32)],
        axis=0,
    )
    mixed_ref[:D, :] = nt(weight_ref[...], mixer_ref[...]).astype(BF)
    if mixed_ref.shape[0] > D:
        mixed_ref[D:, :] = jnp.zeros((mixed_ref.shape[0] - D, rows), BF)
    for key in range(count_ctx):
        spot = pl.multiple_of(jnp.bitwise_xor(scalar_ref[0], key) * width, HEAD_DIM)
        blocks_ref[key] = mixed_ref[pl.ds(spot, width), :]


def unmix(scalars, second, own, other, unit, rate, small, weight, width, count_ctx):
    rows = second.shape[0]
    outs = (
        shape((rows, D), F32),
        shape((rows, D), BF),
        shape((count_ctx, width, rows), BF),
        shape((8, D), F32),
    )

    def body(*refs):
        unmix_kernel((width, count_ctx), *refs)

    return pl.pallas_call(
        body,
        out_shape=outs,
        in_specs=[SMEM] + [VMEM] * 7,
        out_specs=[VMEM] * 4,
        scratch_shapes=[pltpu.VMEM((width * count_ctx, rows), BF)],
        cost_estimate=pl.CostEstimate(
            flops=2 * rows * D * D, bytes_accessed=12_000_000, transcendentals=0
        ),
        name="unmix",
    )(scalars, second, own, other, unit, rate, small, weight)


def spread_fsdp(piece):
    count = lax.axis_size("fsdp")
    pieces = [None] * count
    pieces[0] = piece
    for key in range(2, count, 2):
        pieces[key] = swap(piece, "fsdp", key)
    for key in range(0, count, 2):
        pieces[key + 1] = swap(pieces[key], "fsdp", 1)
    return pieces


def tree_sum(terms):
    while len(terms) > 1:
        terms = [terms[i] + terms[i + 1] for i in range(0, len(terms), 2)]
    return terms[0]


def pick(block, index, axis):
    return lax.dynamic_index_in_dim(block, index, axis, keepdims=False)


def gather_back(share, axis, index, keys):
    pieces = {0: share}
    for key in keys:
        pieces[key] = swap(share, axis, key)
    return pieces


def reduce_fsdp(block):
    count = block.shape[0]
    own = lax.axis_index("fsdp")
    rest = block.shape[1:]
    pairs = block.reshape((count // 2, 2) + rest)
    kept = pick(pairs, own % 2, 1)
    came = swap(pick(pairs, 1 - own % 2, 1), "fsdp", 1)
    column = (kept.astype(F32) + came.astype(F32)).astype(BF)
    place = own // 2
    terms = [pick(column, place, 0).astype(F32)]
    for key in range(1, count // 2):
        terms.append(swap(pick(column, place ^ key, 0), "fsdp", 2 * key).astype(F32))
    return tree_sum(terms)


def reduce_rows(block):
    count, rows, columns = block.shape
    chips = lax.axis_size("ctx") // 2
    place = lax.axis_index("ctx") // 2
    parts = block.reshape(count, chips, rows // chips, columns)
    terms = [pick(parts, place, 1).astype(F32)]
    for key in range(1, chips):
        terms.append(swap(pick(parts, place ^ key, 1), "ctx", 2 * key).astype(F32))
    total = reduce_fsdp(tree_sum(terms).astype(BF)).astype(BF)
    pieces = [total]
    for key in range(1, chips):
        pieces.append(swap(total, "ctx", 2 * key))
    stacked = jnp.stack(pieces)
    ordered = stacked[jnp.arange(chips) ^ place] if chips > 2 else by_bit(stacked, place)
    return ordered.reshape(rows, columns)


def by_bit(stacked, bit):
    return jnp.where(bit == 0, stacked, stacked[::-1])


def per_device(
    tokens,
    cotangent,
    lengths,
    w_query,
    w_key,
    w_value,
    w_out,
    w_up,
    w_down,
    b_query,
    b_value,
    b_out,
    b_up,
    b_down,
    gain_first,
    shift_first,
    gain_second,
    shift_second,
    conv_taps,
):
    own_tokens = tokens[0]
    rows = own_tokens.shape[0]
    count_ctx = lax.axis_size("ctx")
    count_fsdp = lax.axis_size("fsdp")
    own_ctx = lax.axis_index("ctx")
    own_fsdp = lax.axis_index("fsdp")
    core = own_ctx % 2
    length = lengths[0]
    heads = -(-HEADS // count_ctx)
    width = heads * HEAD_DIM
    shard = w_query.shape[0]
    share = w_down.shape[0] // 2
    scalars = jnp.stack([own_ctx, own_fsdp, length, length]).astype(jnp.int32)

    token_pieces = [own_tokens]
    for key in range(2, count_ctx, 2):
        token_pieces += [None, swap(own_tokens, "ctx", key)]
    token_pieces.append(None)
    for key in range(0, count_ctx, 2):
        token_pieces[key + 1] = swap(token_pieces[key], "ctx", 1)

    def own_columns(weight):
        weight = jnp.pad(weight, ((0, 0), (0, width * count_ctx - D)))
        return lax.dynamic_slice_in_dim(weight, own_ctx * width, width, 1)

    vectors = jnp.stack(
        [b_query, b_value, b_out, b_down, gain_first, shift_first, gain_second, shift_second]
    )
    vectors = jnp.concatenate(
        [
            jnp.pad(vectors, ((0, 0), (0, 128 - shard))),
            jnp.pad(b_up[None, :], ((0, 7), (0, 3 * width - 128 - b_up.shape[0]))),
        ],
        axis=1,
    )
    qkv_piece = jnp.concatenate(
        [
            jnp.concatenate([own_columns(w) for w in (w_query, w_key, w_value)], axis=1),
            vectors,
        ],
        axis=0,
    ).astype(BF)
    qkv_pieces = spread_fsdp(qkv_piece)
    own_up = pick(w_up.reshape(shard, count_fsdp, 2, share), core, 2).reshape(shard, FF // 2)
    up_piece = jnp.concatenate([own_up, w_out], axis=1).astype(BF)
    down_piece = pick(w_down.reshape(2, share, D), core, 0).astype(BF)
    up_piece, down_piece, *_ = lax.optimization_barrier((up_piece, down_piece, *qkv_pieces))
    up_pieces = spread_fsdp(up_piece)
    down_pieces = spread_fsdp(down_piece)

    own_taps = lax.dynamic_slice_in_dim(
        jnp.pad(conv_taps, ((0, heads * count_ctx - HEADS), (0, 0))), own_ctx * heads, heads, 0
    )
    ahead, behind = taps_bands(own_taps)

    sequence, turned, qkv, small, land, state, blocks = attend(
        scalars, token_pieces, qkv_pieces, ahead, heads, rows, shard
    )
    small = small.reshape(count_fsdp, 8, 3 * width)
    vectors = small[:, :, :shard].transpose(1, 0, 2).reshape(8, D).astype(F32)
    up_bias = small[:, 0, 128 : 128 + 2 * share].reshape(count_fsdp, 2, share)
    up_bias = pick(up_bias, core, 1).reshape(1, FF // 2).astype(F32)
    up_bias = jnp.broadcast_to(up_bias, (8, FF // 2))

    mixed_pieces = [blocks[0]] + [swap(blocks[k], "ctx", k) for k in range(1, count_ctx)]
    mixed, out_weight, hidden, hidden_low, unit, rate = project(
        scalars, mixed_pieces, up_pieces, own_tokens, vectors, width, shard, FF // 2
    )
    hidden_other = swap(hidden_low, "ctx", 1)
    both, up_weight, down_weight, active, slope, feed = lift(
        scalars, hidden_low, hidden_other, up_pieces, down_pieces, up_bias, shard, share
    )
    feed_other = swap(feed[rows:], "ctx", 1)
    output, d_second, d_feed, second_sums = finish(
        scalars, hidden, feed[:rows], feed_other, vectors, cotangent[0]
    )
    d_feed_other = swap(d_feed, "ctx", 1)
    d_feed_both, d_lifted, d_hidden, d_up_bias = lower(
        d_feed, d_feed_other, slope, up_weight, down_weight
    )
    d_hidden_other = swap(d_hidden[rows:], "ctx", 1)
    grad_down = jnp.einsum("tf,td->fd", active, d_feed_both, preferred_element_type=F32).astype(BF)
    grad_up = jnp.einsum("td,tf->df", both, d_lifted, preferred_element_type=F32).astype(BF)
    d_first, d_mixer, d_blocks, first_sums = unmix(
        scalars,
        d_second,
        d_hidden[:rows],
        d_hidden_other,
        unit,
        rate,
        vectors,
        out_weight,
        width,
        count_ctx,
    )
    grad_out = jnp.dot(mixed[:D], d_mixer, preferred_element_type=F32).astype(BF)

    grad_pieces = [d_blocks[0]] + [swap(d_blocks[k], "ctx", k) for k in range(1, count_ctx)]
    qkv_share, near_keep, near_send = attend_back(
        scalars,
        grad_pieces,
        (sequence, turned, qkv, land, state),
        behind,
        heads,
        rows,
        shard,
        count_fsdp,
    )

    down_total = reduce_rows(grad_down.reshape(count_fsdp, share, D))
    out_halves = grad_out.reshape(count_fsdp, shard, 2, D // 2)
    out_half = pick(out_halves, core, 2).astype(F32) + swap(
        pick(out_halves, 1 - core, 2), "ctx", 1
    ).astype(F32)
    sums = jnp.concatenate([first_sums[:3], second_sums[:3]], axis=0)
    rest = jnp.concatenate(
        [
            jnp.pad(
                d_up_bias[0].reshape(count_fsdp, 1, share),
                ((0, 0), (0, 0), (0, FF // 2 + D // 2 - share)),
            ),
            jnp.pad(
                sums.reshape(6, count_fsdp, shard).transpose(1, 0, 2),
                ((0, 0), (0, 9), (0, FF // 2 + D // 2 - shard)),
            ),
        ],
        axis=1,
    ).astype(BF)
    up_block = jnp.concatenate(
        [grad_up.reshape(count_fsdp, shard, FF // 2), out_half.astype(BF)], axis=2
    )
    up_total = reduce_rows(jnp.concatenate([up_block, rest], axis=1))
    down_other = swap(down_total, "ctx", 1)
    up_other = swap(up_total, "ctx", 1)
    down_both = by_bit(jnp.stack([down_total, down_other]), core)
    up_both = by_bit(jnp.stack([up_total, up_other]), core)
    grad_w_down = down_both.reshape(2 * share, D).astype(F32)
    grad_w_up = (
        up_both[:, :shard, : FF // 2]
        .reshape(2, shard, count_fsdp, share)
        .transpose(1, 2, 0, 3)
        .reshape(shard, FF)
        .astype(F32)
    )
    grad_w_out = up_both[:, :shard, FF // 2 :].transpose(1, 0, 2).reshape(shard, D).astype(F32)
    grad_b_up = up_both[:, shard, :share].reshape(2 * share).astype(F32)
    small_sums = up_both[:, shard + 1 : shard + 7, :shard].astype(F32)
    small_sums = small_sums[0] + small_sums[1]

    qkv_total = reduce_fsdp(qkv_share).astype(BF)
    chips = count_ctx // 2
    totals = [qkv_total] + [swap(qkv_total, "ctx", 2 * key) for key in range(1, chips)]
    stacked = jnp.stack(totals)
    pairs = jnp.stack([stacked, swap(stacked, "ctx", 1)], axis=1)
    pairs = jnp.where(core == 0, pairs, pairs[:, ::-1])
    if chips == 2:
        pairs = by_bit(pairs, own_ctx // 2)
    else:
        pairs = pairs[jnp.arange(chips) ^ (own_ctx // 2)]
    pairs = pairs.reshape(count_ctx, shard + 8, 3 * width)

    def columns(begin):
        part = pairs[:, :shard, begin : begin + width].transpose(1, 0, 2)
        return part.reshape(shard, count_ctx * width)[:, :D].astype(F32)

    grad_w_query, grad_w_key, grad_w_value = columns(0), columns(width), columns(2 * width)
    grad_b_query = jnp.sum(pairs[:, shard, :shard].astype(F32), axis=0)
    grad_b_value = jnp.sum(pairs[:, shard + 1, :shard].astype(F32), axis=0)
    grad_taps = pairs[:, shard + 2 : shard + 2 + heads, :KSIZE].reshape(-1, KSIZE)[:HEADS].astype(F32)

    near = near_keep + swap(near_send, "ctx", 1)
    total = d_first + near[0]
    for key in range(1, chips):
        total = total + swap(near[key].astype(BF), "ctx", 2 * key).astype(F32)
    live = (own_ctx * rows + jnp.arange(rows, dtype=jnp.int32) < length)[:, None]
    input_grad = jnp.where(live, total, 0.0).astype(BF)

    return (
        output[None],
        input_grad[None],
        grad_w_query,
        grad_w_key,
        grad_w_value,
        grad_w_out,
        grad_w_up,
        grad_w_down,
        grad_b_query,
        grad_b_value,
        small_sums[2],
        grad_b_up,
        small_sums[5],
        small_sums[0],
        small_sums[1],
        small_sums[3],
        small_sums[4],
        grad_taps,
    )


def solution(mesh):
    vector = P("fsdp")
    matrix = P("fsdp", None)
    sequence = P("fsdp", "ctx", None)
    return jax.shard_map(
        per_device,
        mesh=mesh,
        in_specs=(sequence, sequence, vector) + (matrix,) * 6 + (vector,) * 9 + (P(),),
        out_specs=(sequence, sequence) + (matrix,) * 6 + (vector,) * 9 + (P(),),
        check_vma=False,
    )
```

time: 1070 us -> 386 us (0.36)
  waiting for transfers between devices: 517 us -> 127 us
  matrix products: 148 us -> 8.75 us
  blocking collectives: 135 us -> 0 us
  local copies, waits for them, and re-layouts: 153 us -> 47.6 us
  Pallas kernels: 0 us -> 79.5 us
  starting transfers between devices: 19 us -> 89.3 us
  other arithmetic: 73.3 us -> 24.1 us
  between operations: 20.8 us -> 2.06 us
    reduce_scatter x3 -> x0, waiting for transfers between devices: 264 us -> none  [the longest x1 100 us: per_device(): lax.psum_scatter(grad_up.astype(jnp.bfloat16), 'fsdp', scatter_dimension=...]
    all_gather x8 -> x0, waiting for transfers between devices: 210 us -> none  [the longest x1 67.7 us: per_device(): lax.all_gather(w_down.astype(jnp.bfloat16), 'fsdp', axis=0, tiled=True)]
    dot_general x111 -> x3, matrix products: 145 us -> 8.75 us  [the longest x1 4.46 us: per_device(): jnp.einsum('td,tf->df', both, d_lifted, preferred_element_type=F32)]
    ppermute x4 -> x57, waiting for transfers between devices: 0.01 us -> 127 us  [swap(): return lax.ppermute(block, axis, [(i, i ^ key) for i in range(count)])]
    pallas_call x0 -> x8, Pallas kernels: none -> 79.5 us  [the longest x1 23.4 us: attend_back(): pl.pallas_call(body, out_shape=outs, in_specs=[SMEM] + [ANY] * count_ctx...]
    ppermute x4 -> x57, starting transfers between devices: 17.9 us -> 89.3 us  [swap(): return lax.ppermute(block, axis, [(i, i ^ key) for i in range(count)])]
    convert_element_type x37 -> x16, local copies, waits for them, and re-layouts: 72.7 us -> 11.5 us  [the longest x3 4.33 us: per_device(): grad_w_up = up_both[:, :shard, :FF // 2].reshape(2, shard, count_fsdp, sh...]
    unnamed x2 -> x0, blocking collectives: 60.7 us -> none
  transfers between devices with their start and end apart: 21 -> 57, of which waited for: 9 -> 24; matrix products, arithmetic and copies ran while one was open for 26% -> 15% of each run, Pallas kernels for 0% -> 14%
where the time goes in v1:
time: 386 us; the launch traced here: 378 us
  waiting for transfers between devices  127 us (33%)
  starting transfers between devices  89.3 us (23%)
  Pallas kernels  79.5 us (21%)
  local copies, waits for them, and re-layouts  47.6 us (12%)
  other arithmetic  24.1 us (6%)
  matrix products  8.75 us (2%)
    ppermute x57, waiting for transfers between devices, swap(): return lax.ppermute(block, axis, [(i, i ^ key) for i in range(count)])  127 us
    ppermute x57, starting transfers between devices, swap(): return lax.ppermute(block, axis, [(i, i ^ key) for i in range(count)])  89.3 us
    pallas_call x1, Pallas kernels, attend_back(): pl.pallas_call(body, out_shape=outs, in_specs=[SMEM] + [ANY] * count_ctx...  23.4 us
    pallas_call x1, Pallas kernels, attend(): pl.pallas_call(body, out_shape=outs, in_specs=[SMEM] + [ANY] * (count_ctx...  16.6 us
    pallas_call x1, Pallas kernels, lower(): pl.pallas_call(lower_kernel, out_shape=outs, in_specs=[VMEM] * 5, out_spe...  11.6 us
    pallas_call x1, Pallas kernels, lift(): pl.pallas_call(body, out_shape=outs, in_specs=[SMEM, VMEM, VMEM] + [ANY]...  10.7 us
  transfers between devices with their start and end apart: 57, of which 24 were waited for; matrix products, arithmetic and copies ran while one was open for 15% of the time, Pallas kernels for 14%

profile of v1, /device:TPU:1, one launch (start us, length us, event | category | flops | bytes accessed | tf_op | source)
XLA Modules:
  0.0 378.4 jit_solution(17458783856118177621)
XLA Ops:
  21.5 3.9 %collective-permute-start = (bf16[256,768]{1,0:T(8,128)(2,1)S(1)}, bf16[256,768]{1,0:T(8,128)(2,1)}, u32[]{:S(2)}, u32[]{:S(2)}) collective-permute-start(bf16[256,768]{1,0:T(8,128)(2,1)S(1)} %bitcast.216), channel_id=1, source_target_pairs={{0,8},{8,0},{16,24},{24,16},{1,9},{9,1},{17,25},{25,17},{2,10},{10... | collective-permute-start | bytes 1179656 | tf_op jit(solution)/shard_map/ppermute | solution.py:51
  40.3 4.2 %collective-permute-done.14.refs_7_.refs_5_ = bf16[96,2304]{1,0:T(8,128)(2,1)S(1)} collective-permute-done((bf16[96,2304]{1,0:T(8,128)(2,1)S(1)}, bf16[96,2304]{1,0:T(8,128)(2,1)S(1)}, u32[]{:S(2)}, u32[]{:S(2)}) %collective-permute-start.14) | collective-permute-done | bytes 442400 | tf_op jit(solution)/shard_map/ppermute | solution.py:51
  46.7 11.0 %collective-permute-done.18.refs_11_.refs_9_ = bf16[96,2304]{1,0:T(8,128)(2,1)S(1)} collective-permute-done((bf16[96,2304]{1,0:T(8,128)(2,1)S(1)}, bf16[96,2304]{1,0:T(8,128)(2,1)S(1)}, u32[]{:S(2)}, u32[]{:S(2)}) %collective-permute-start.18) | collective-permute-done | bytes 442400 | tf_op jit(solution)/shard_map/ppermute | solution.py:51
  57.8 16.6 %attend.1 = (bf16[1024,768]{1,0:T(8,128)(2,1)}, bf16[576,768]{1,0:T(8,128)(2,1)}, bf16[576,1024]{1,0:T(8,128)(2,1)}, bf16[64,576]{1,0:T(8,128)(2,1)}, f32[6,3,64...) custom-call(s32[4]{0:T(128)} %pad_add_fusion.refs_0_.scalar_ref, ...), custom_call_target="tpu_custom_call" | custom-call | flops 1811939328 | bytes 60000000 | tf_op jit(solution)/shard_map/attend/pallas_call | solution.py:278
  76.2 7.5 %collective-permute-start.10 = (bf16[192,256]{1,0:T(8,128)(2,1)S(1)}, bf16[192,256]{1,0:T(8,128)(2,1)S(1)}, u32[]{:S(2)}, u32[]{:S(2)}) collective-permute-start(bf16[192,256]{1,0:T(8,128)(2,1)S(1)} %get-tuple-element.120), channel_id=1, source_target_pairs={{0,8},{8,0},{16,24},{24,16},{1,9},{9,1},{17,25},{25,17},{2,10},{10... | collective-permute-start | bytes 294920 | tf_op jit(solution)/shard_map/ppermute | solution.py:51
  88.0 6.3 %collective-permute-start.22 = (bf16[192,768]{1,0:T(8,128)(2,1)S(1)}, bf16[192,768]{1,0:T(8,128)(2,1)}, u32[]{:S(2)}, u32[]{:S(2)}) collective-permute-start(bf16[192,768]{1,0:T(8,128)(2,1)S(1)} %copy-done.22), channel_id=1, source_target_pairs={{0,2},{1,3},{2,0},{3,1},{4,6},{5,7},{6,4},{7,5},{8,10},{9,11},{10,... | collective-permute-start | bytes 884744 | tf_op jit(solution)/shard_map/ppermute | solution.py:51
  94.3 3.3 collective-permute-start.24
  100.2 5.6 %project.1 = (bf16[768,256]{1,0:T(8,128)(2,1)}, bf16[768,768]{1,0:T(8,128)(2,1)}, f32[256,768]{1,0:T(8,128)}, bf16[256,768]{1,0:T(8,128)(2,1)}, f32[256,768]{1,0:T(8,128)}, /*index=5*/f32[256,128]{1,0:T(8,128)}) custom-call(s32[4]{0:T(128)} %pad_add_fusion.refs_0_.scalar_ref, bf16[192,256]{1,0:T(8,128)(2,1)} %get-tuple-element.121.refs_1_, ...), custom_call_target="tpu_custom_call" | custom-call | flops 301989888 | bytes 12000000 | tf_op jit(solution)/shard_map/project/pallas_call | solution.py:595
  108.6 6.3 %collective-permute-done.26.refs_17_ = bf16[192,768]{1,0:T(8,128)(2,1)} collective-permute-done((bf16[192,768]{1,0:T(8,128)(2,1)S(1)}, bf16[192,768]{1,0:T(8,128)(2,1)}, u32[]{:S(2)}, u32[]{:S(2)}) %collective-permute-start.26) | collective-permute-done | bytes 294944 | tf_op jit(solution)/shard_map/ppermute | solution.py:51
  116.4 5.1 %collective-permute-done.23.refs_14_ = bf16[192,768]{1,0:T(8,128)(2,1)S(1)} collective-permute-done((bf16[192,768]{1,0:T(8,128)(2,1)}, bf16[192,768]{1,0:T(8,128)(2,1)S(1)}, u32[]{:S(2)}, u32[]{:S(2)}) %collective-permute-start.23) | collective-permute-done | bytes 294944 | tf_op jit(solution)/shard_map/ppermute | solution.py:51
  121.5 5.9 %collective-permute-done.25.refs_16_ = bf16[192,768]{1,0:T(8,128)(2,1)S(1)} collective-permute-done((bf16[192,768]{1,0:T(8,128)(2,1)}, bf16[192,768]{1,0:T(8,128)(2,1)S(1)}, u32[]{:S(2)}, u32[]{:S(2)}) %collective-permute-start.25) | collective-permute-done | bytes 294944 | tf_op jit(solution)/shard_map/ppermute | solution.py:51
  127.4 6.3 %collective-permute-done.27.refs_18_ = bf16[192,768]{1,0:T(8,128)(2,1)S(1)} collective-permute-done((bf16[192,768]{1,0:T(8,128)(2,1)}, bf16[192,768]{1,0:T(8,128)(2,1)S(1)}, u32[]{:S(2)}, u32[]{:S(2)}) %collective-permute-start.27) | collective-permute-done | bytes 294944 | tf_op jit(solution)/shard_map/ppermute | solution.py:51
  134.6 10.7 %lift.1 = (bf16[512,768]{1,0:T(8,128)(2,1)}, bf16[768,1536]{1,0:T(8,128)(2,1)}, bf16[1536,768]{1,0:T(8,128)(2,1)}, bf16[512,1536]{1,0:T(8,128)(2,1)}, f32[512,1536]{1,0:T(8,128)}, /*index=5*/f32[512,768]{1,0:T(8,128)}) custom-call(s32[4]{0:T(128)} %pad_add_fusion.refs_0_.scalar_ref, bf16[256,768]{1,0:T(8,128)(2,1)} %get-tuple-element.61.refs_1_, ...), custom_call_target="tpu_custom_call" | custom-call | flops 4831838208 | bytes 40000000 | tf_op jit(solution)/shard_map/lift/pallas_call | solution.py:681
  151.9 4.2 %finish.1 = (bf16[256,768]{1,0:T(8,128)(2,1)}, f32[256,768]{1,0:T(8,128)}, bf16[256,768]{1,0:T(8,128)(2,1)}, f32[8,768]{1,0:T(8,128)}) custom-call(s32[4]{0:T(128)} %pad_add_fusion.refs_0_.scalar_ref, f32[256,768]{1,0:T(8,128)} %get-tuple-element.60.hidden_ref, f32[256,768]{1,0:T(8,128)} %get-tuple-element.99.own_ref, f32[256,768]{1,0:T(8,128)} %copy-done.12, ...), custom_call_target="tpu_custom_call" | custom-call | flops 5898240 | bytes 9000000 | tf_op jit(solution)/shard_map/finish/pallas_call | solution.py:757
  158.7 11.6 %lower.1 = (bf16[512,768]{1,0:T(8,128)(2,1)}, bf16[512,1536]{1,0:T(8,128)(2,1)}, f32[512,768]{1,0:T(8,128)}, f32[8,1536]{1,0:T(8,128)}) custom-call(bf16[256,768]{1,0:T(8,128)(2,1)} %get-tuple-element.66.own_ref, bf16[256,768]{1,0:T(8,128)(2,1)} %copy-done.28, f32[512,1536]{1,0:T(8,128)} %get-tuple-element.67.slope_ref, ...), custom_call_target="tpu_custom_call" | custom-call | flops 4831838208 | bytes 30000000 | tf_op jit(solution)/shard_map/lower/pallas_call | solution.py:796
  180.3 4.5 %convolution_convert_fusion.1 = bf16[768,1536]{1,0:T(8,128)(2,1)} fusion(bf16[512,768]{1,0:T(8,128)(2,1)} %get-tuple-element.85, bf16[512,1536]{1,0:T(8,128)(2,1)} %get-tuple-element.86), kind=kOutput, calls=%fused_computation.11 | convolution fusion | flops 1209139200 | bytes 4718592 | tf_op jit(solution)/shard_map/td,tf->df/dot_general | solution.py:1057
  185.6 4.4 %unmix.1 = (f32[256,768]{1,0:T(8,128)}, bf16[256,768]{1,0:T(8,128)(2,1)}, bf16[4,192,256]{2,1,0:T(8,128)(2,1)}, f32[8,768]{1,0:T(8,128)}) custom-call(s32[4]{0:T(128)} %pad_add_fusion.refs_0_.scalar_ref, f32[256,768]{1,0:T(8,128)} %get-tuple-element.65.refs_1_, f32[256,768]{1,0:T(8,128)} %get-tuple-element.97.refs_2_, f32[256,768]{1,0:T(8,128)} %copy-done.11, ...), custom_call_target="tpu_custom_call" | custom-call | flops 301989888 | bytes 12000000 | tf_op jit(solution)/shard_map/unmix/pallas_call | solution.py:877
  199.5 7.5 %collective-permute-done.32.refs_3_ = bf16[192,256]{1,0:T(8,128)(2,1)S(1)} collective-permute-done((bf16[192,256]{1,0:T(8,128)(2,1)S(1)}, bf16[192,256]{1,0:T(8,128)(2,1)S(1)}, u32[]{:S(2)}, u32[]{:S(2)}) %collective-permute-start.32) | collective-permute-done | bytes 98336 | tf_op jit(solution)/shard_map/ppermute | solution.py:51
  210.0 23.4 %attend_back.1 = (bf16[8,104,576]{2,1,0:T(8,128)(2,1)}, f32[2,256,768]{2,1,0:T(8,128)}, f32[2,256,768]{2,1,0:T(8,128)}) custom-call(s32[4]{0:T(128)} %pad_add_fusion.refs_0_.scalar_ref, bf16[192,256]{1,0:T(8,128)(2,1)} %get-tuple-element.117.refs_1_, bf16[192,256]{1,0:T(8,128)(2,1)} %copy-done.41, bf16[192,256]{1,0:T(8,128)(2,1)} %copy-done.42, ...), custom_call_target="tpu_custom_call" | custom-call | flops 3623878656 | bytes 100000000 | tf_op jit(solution)/shard_map/attend_back/pallas_call | solution.py:504
  241.2 8.0 %collective-permute-done.36 = bf16[4,104,576]{2,1,0:T(8,128)(2,1)} collective-permute-done((bf16[4,104,576]{2,1,0:T(8,128)(2,1)}, bf16[4,104,576]{2,1,0:T(8,128)(2,1)}, u32[]{:S(2)}, u32[]{:S(2)}) %collective-permute-start.36) | collective-permute-done | bytes 479264 | tf_op jit(solution)/shard_map/ppermute | solution.py:51
  257.2 3.3 collective-permute-done.39
  262.5 4.4 %collective-permute-start.34 = (f32[2,256,768]{2,1,0:T(8,128)}, f32[2,256,768]{2,1,0:T(8,128)}, u32[]{:S(2)}, u32[]{:S(2)}) collective-permute-start(f32[2,256,768]{2,1,0:T(8,128)} %get-tuple-element.83), channel_id=1, source_target_pairs={{0,8},{8,0},{16,24},{24,16},{1,9},{9,1},{17,25},{25,17},{2,10},{10... | collective-permute-start | bytes 4718600 | tf_op jit(solution)/shard_map/ppermute | solution.py:51
  266.9 29.0 %collective-permute-done.40 = bf16[104,576]{1,0:T(8,128)(2,1)} collective-permute-done((bf16[104,576]{1,0:T(8,128)(2,1)}, bf16[104,576]{1,0:T(8,128)(2,1)}, u32[]{:S(2)}, u32[]{:S(2)}) %collective-permute-start.40) | collective-permute-done | bytes 119840 | tf_op jit(solution)/shard_map/ppermute | solution.py:51
  296.9 3.2 collective-permute-start.41
  305.5 4.3 %collective-permute-done.52 = bf16[96,768]{1,0:T(8,128)(2,1)S(1)} collective-permute-done((bf16[96,768]{1,0:T(8,128)(2,1)S(1)}, bf16[96,768]{1,0:T(8,128)(2,1)S(1)}, u32[]{:S(2)}, u32[]{:S(2)}) %collective-permute-start.52) | collective-permute-done | bytes 147488 | tf_op jit(solution)/shard_map/ppermute | solution.py:51
  309.8 4.5 %collective-permute-done.54 = bf16[96,768]{1,0:T(8,128)(2,1)S(1)} collective-permute-done((bf16[96,768]{1,0:T(8,128)(2,1)S(1)}, bf16[96,768]{1,0:T(8,128)(2,1)S(1)}, u32[]{:S(2)}, u32[]{:S(2)}) %collective-permute-start.54) | collective-permute-done | bytes 147488 | tf_op jit(solution)/shard_map/ppermute | solution.py:51
  328.6 8.7 %collective-permute-done.44 = bf16[4,56,1920]{2,1,0:T(8,128)(2,1)} collective-permute-done((bf16[4,56,1920]{2,1,0:T(8,128)(2,1)S(1)}, bf16[4,56,1920]{2,1,0:T(8,128)(2,1)}, u32[]{:S(2)}, u32[]{:S(2)}) %collective-permute-start.44) | collective-permute-done | bytes 860192 | tf_op jit(solution)/shard_map/ppermute | solution.py:51
  338.7 4.2 %collective-permute-start.45 = (bf16[56,1920]{1,0:T(8,128)(2,1)S(1)}, bf16[56,1920]{1,0:T(8,128)(2,1)S(1)}, u32[]{:S(2)}, u32[]{:S(2)}) collective-permute-start(bf16[56,1920]{1,0:T(8,128)(2,1)S(1)} %get-tuple-element.102), channel_id=1, source_target_pairs={{0,2},{1,3},{2,0},{3,1},{4,6},{5,7},{6,4},{7,5},{8,10},{9,11},{10,... | collective-permute-start | bytes 645128 | tf_op jit(solution)/shard_map/ppermute | solution.py:51
  346.9 3.3 collective-permute-done.46
  350.2 7.1 %collective-permute-done.47 = bf16[56,1920]{1,0:T(8,128)(2,1)S(1)} collective-permute-done((bf16[56,1920]{1,0:T(8,128)(2,1)S(1)}, bf16[56,1920]{1,0:T(8,128)(2,1)S(1)}, u32[]{:S(2)}, u32[]{:S(2)}) %collective-permute-start.47) | collective-permute-done | bytes 215072 | tf_op jit(solution)/shard_map/ppermute | solution.py:51
  359.1 3.4 collective-permute-done.48
  362.6 7.0 %collective-permute-start.49 = (bf16[112,1920]{1,0:T(8,128)(2,1)S(1)}, bf16[112,1920]{1,0:T(8,128)(2,1)S(1)}, u32[]{:S(2)}, u32[]{:S(2)}) collective-permute-start(bf16[112,1920]{1,0:T(8,128)(2,1)S(1)} %bitcast.204), channel_id=1, source_target_pairs={{0,8},{8,0},{16,24},{24,16},{1,9},{9,1},{17,25},{25,17},{2,10},{10... | collective-permute-start | bytes 1290248 | tf_op jit(solution)/shard_map/ppermute | solution.py:51
  (289 shorter events, 137.4 us)
Async XLA Ops:
  6.4 11.2 %collective-permute-start.4 = (bf16[104,576]{1,0:T(8,128)(2,1)S(1)}, bf16[104,576]{1,0:T(8,128)(2,1)S(1)}, u32[]{:S(2)}, u32[]{:S(2)}) collective-permute-start(bf16[104,576]{1,0:T(8,128)(2,1)S(1)} %fusion.31.refs_5_), channel_id=1, source_target_pairs={{0,2},{1,3},{2,0},{3,1},{4,6},{5,7},{6,4},{7,5},{8,10},{9,11},{10,... | collective-permute-start | bytes 359432 | tf_op jit(solution)/shard_map/ppermute | solution.py:51
  10.9 10.6 %collective-permute-start.3 = (bf16[104,576]{1,0:T(8,128)(2,1)S(1)}, bf16[104,576]{1,0:T(8,128)(2,1)S(1)}, u32[]{:S(2)}, u32[]{:S(2)}) collective-permute-start(bf16[104,576]{1,0:T(8,128)(2,1)S(1)} %fusion.31.refs_5_), channel_id=1, source_target_pairs={{0,1},{1,0},{2,3},{3,2},{4,5},{5,4},{6,7},{7,6},{8,9},{9,8},{10,11... | collective-permute-start | bytes 359432 | tf_op jit(solution)/shard_map/ppermute | solution.py:51
  12.1 18.8 %collective-permute-start.1 = (bf16[256,768]{1,0:T(8,128)(2,1)}, bf16[256,768]{1,0:T(8,128)(2,1)}, u32[]{:S(2)}, u32[]{:S(2)}) collective-permute-start(bf16[256,768]{1,0:T(8,128)(2,1)} %bitcast.213), channel_id=1, source_target_pairs={{0,16},{8,24},{16,0},{24,8},{1,17},{9,25},{17,1},{25,9},{2,18},{10... | collective-permute-start | bytes 1179656 | tf_op jit(solution)/shard_map/ppermute | solution.py:51
  21.5 18.0 %collective-permute-start = (bf16[256,768]{1,0:T(8,128)(2,1)S(1)}, bf16[256,768]{1,0:T(8,128)(2,1)}, u32[]{:S(2)}, u32[]{:S(2)}) collective-permute-start(bf16[256,768]{1,0:T(8,128)(2,1)S(1)} %bitcast.216), channel_id=1, source_target_pairs={{0,8},{8,0},{16,24},{24,16},{1,9},{9,1},{17,25},{25,17},{2,10},{10... | collective-permute-start | bytes 1179656 | tf_op jit(solution)/shard_map/ppermute | solution.py:51
  26.4 18.1 %collective-permute-start.14 = (bf16[96,2304]{1,0:T(8,128)(2,1)S(1)}, bf16[96,2304]{1,0:T(8,128)(2,1)S(1)}, u32[]{:S(2)}, u32[]{:S(2)}) collective-permute-start(bf16[96,2304]{1,0:T(8,128)(2,1)S(1)} %pad_maximum_fusion.3.refs_5_.refs_3_), channel_id=1, source_target_pairs={{0,2},{1,3},{2,0},{3,1},{4,6},{5,7},{6,4},{7,5},{8,10},{9,11},{10,... | collective-permute-start | bytes 1327112 | tf_op jit(solution)/shard_map/ppermute | solution.py:51
  28.2 17.6 %collective-permute-start.16 = (bf16[96,2304]{1,0:T(8,128)(2,1)S(1)}, bf16[96,2304]{1,0:T(8,128)(2,1)S(1)}, u32[]{:S(2)}, u32[]{:S(2)}) collective-permute-start(bf16[96,2304]{1,0:T(8,128)(2,1)S(1)} %pad_maximum_fusion.3.refs_5_.refs_3_), channel_id=1, source_target_pairs={{0,4},{1,5},{2,6},{3,7},{4,0},{5,1},{6,2},{7,3},{8,12},{9,13},{10,... | collective-permute-start | bytes 1327112 | tf_op jit(solution)/shard_map/ppermute | solution.py:51
  29.9 27.8 %collective-permute-start.18 = (bf16[96,2304]{1,0:T(8,128)(2,1)S(1)}, bf16[96,2304]{1,0:T(8,128)(2,1)S(1)}, u32[]{:S(2)}, u32[]{:S(2)}) collective-permute-start(bf16[96,2304]{1,0:T(8,128)(2,1)S(1)} %pad_maximum_fusion.3.refs_5_.refs_3_), channel_id=1, source_target_pairs={{0,6},{1,7},{2,4},{3,5},{4,2},{5,3},{6,0},{7,1},{8,14},{9,15},{10,... | collective-permute-start | bytes 1327112 | tf_op jit(solution)/shard_map/ppermute | solution.py:51
  30.9 26.8 %collective-permute-start.2 = (bf16[256,768]{1,0:T(8,128)(2,1)}, bf16[256,768]{1,0:T(8,128)(2,1)}, u32[]{:S(2)}, u32[]{:S(2)}) collective-permute-start(bf16[256,768]{1,0:T(8,128)(2,1)} %collective-permute-done.1.refs_3_), channel_id=1, source_target_pairs={{0,8},{8,0},{16,24},{24,16},{1,9},{9,1},{17,25},{25,17},{2,10},{10... | collective-permute-start | bytes 1179656 | tf_op jit(solution)/shard_map/ppermute | solution.py:51
  39.5 44.2 %collective-permute-start.13 = (bf16[96,2304]{1,0:T(8,128)(2,1)S(1)}, bf16[96,2304]{1,0:T(8,128)(2,1)S(1)}, u32[]{:S(2)}, u32[]{:S(2)}) collective-permute-start(bf16[96,2304]{1,0:T(8,128)(2,1)S(1)} %pad_maximum_fusion.3.refs_5_.refs_3_), channel_id=1, source_target_pairs={{0,1},{1,0},{2,3},{3,2},{4,5},{5,4},{6,7},{7,6},{8,9},{9,8},{10,11... | collective-permute-start | bytes 1327112 | tf_op jit(solution)/shard_map/ppermute | solution.py:51
  44.5 53.1 %collective-permute-start.15 = (bf16[96,2304]{1,0:T(8,128)(2,1)S(1)}, bf16[96,2304]{1,0:T(8,128)(2,1)S(1)}, u32[]{:S(2)}, u32[]{:S(2)}) collective-permute-start(bf16[96,2304]{1,0:T(8,128)(2,1)S(1)} %collective-permute-done.14.refs_7_.refs_5_), channel_id=1, source_target_pairs={{0,1},{1,0},{2,3},{3,2},{4,5},{5,4},{6,7},{7,6},{8,9},{9,8},{10,11... | collective-permute-start | bytes 1327112 | tf_op jit(solution)/shard_map/ppermute | solution.py:51
  45.8 53.6 %collective-permute-start.17 = (bf16[96,2304]{1,0:T(8,128)(2,1)S(1)}, bf16[96,2304]{1,0:T(8,128)(2,1)S(1)}, u32[]{:S(2)}, u32[]{:S(2)}) collective-permute-start(bf16[96,2304]{1,0:T(8,128)(2,1)S(1)} %collective-permute-done.16.refs_9_.refs_7_), channel_id=1, source_target_pairs={{0,1},{1,0},{2,3},{3,2},{4,5},{5,4},{6,7},{7,6},{8,9},{9,8},{10,11... | collective-permute-start | bytes 1327112 | tf_op jit(solution)/shard_map/ppermute | solution.py:51
  57.7 41.7 %collective-permute-start.19 = (bf16[96,2304]{1,0:T(8,128)(2,1)S(1)}, bf16[96,2304]{1,0:T(8,128)(2,1)}, u32[]{:S(2)}, u32[]{:S(2)}) collective-permute-start(bf16[96,2304]{1,0:T(8,128)(2,1)S(1)} %collective-permute-done.18.refs_11_.refs_9_), channel_id=1, source_target_pairs={{0,1},{1,0},{2,3},{3,2},{4,5},{5,4},{6,7},{7,6},{8,9},{9,8},{10,11... | collective-permute-start | bytes 1327112 | tf_op jit(solution)/shard_map/ppermute | solution.py:51
  88.0 19.1 %collective-permute-start.22 = (bf16[192,768]{1,0:T(8,128)(2,1)S(1)}, bf16[192,768]{1,0:T(8,128)(2,1)}, u32[]{:S(2)}, u32[]{:S(2)}) collective-permute-start(bf16[192,768]{1,0:T(8,128)(2,1)S(1)} %copy-done.22), channel_id=1, source_target_pairs={{0,2},{1,3},{2,0},{3,1},{4,6},{5,7},{6,4},{7,5},{8,10},{9,11},{10,... | collective-permute-start | bytes 884744 | tf_op jit(solution)/shard_map/ppermute | solution.py:51
  94.3 13.8 %collective-permute-start.24 = (bf16[192,768]{1,0:T(8,128)(2,1)S(1)}, bf16[192,768]{1,0:T(8,128)(2,1)}, u32[]{:S(2)}, u32[]{:S(2)}) collective-permute-start(bf16[192,768]{1,0:T(8,128)(2,1)S(1)} %copy-done.22), channel_id=1, source_target_pairs={{0,4},{1,5},{2,6},{3,7},{4,0},{5,1},{6,2},{7,3},{8,12},{9,13},{10,... | collective-permute-start | bytes 884744 | tf_op jit(solution)/shard_map/ppermute | solution.py:51
  97.6 17.3 %collective-permute-start.26 = (bf16[192,768]{1,0:T(8,128)(2,1)S(1)}, bf16[192,768]{1,0:T(8,128)(2,1)}, u32[]{:S(2)}, u32[]{:S(2)}) collective-permute-start(bf16[192,768]{1,0:T(8,128)(2,1)S(1)} %copy-done.22), channel_id=1, source_target_pairs={{0,6},{1,7},{2,4},{3,5},{4,2},{5,3},{6,0},{7,1},{8,14},{9,15},{10,... | collective-permute-start | bytes 884744 | tf_op jit(solution)/shard_map/ppermute | solution.py:51
  105.9 27.8 %collective-permute-start.20 = (bf16[256,768]{1,0:T(8,128)(2,1)}, bf16[256,768]{1,0:T(8,128)(2,1)S(1)}, u32[]{:S(2)}, u32[]{:S(2)}) collective-permute-start(bf16[256,768]{1,0:T(8,128)(2,1)} %get-tuple-element.61.refs_1_), channel_id=1, source_target_pairs={{0,8},{8,0},{16,24},{24,16},{1,9},{9,1},{17,25},{25,17},{2,10},{10... | collective-permute-start | bytes 1179656 | tf_op jit(solution)/shard_map/ppermute | solution.py:51
  107.1 14.4 %collective-permute-start.23 = (bf16[192,768]{1,0:T(8,128)(2,1)}, bf16[192,768]{1,0:T(8,128)(2,1)S(1)}, u32[]{:S(2)}, u32[]{:S(2)}) collective-permute-start(bf16[192,768]{1,0:T(8,128)(2,1)} %collective-permute-done.22.refs_13_), channel_id=1, source_target_pairs={{0,1},{1,0},{2,3},{3,2},{4,5},{5,4},{6,7},{7,6},{8,9},{9,8},{10,11... | collective-permute-start | bytes 884744 | tf_op jit(solution)/shard_map/ppermute | solution.py:51
  108.1 19.3 %collective-permute-start.25 = (bf16[192,768]{1,0:T(8,128)(2,1)}, bf16[192,768]{1,0:T(8,128)(2,1)S(1)}, u32[]{:S(2)}, u32[]{:S(2)}) collective-permute-start(bf16[192,768]{1,0:T(8,128)(2,1)} %collective-permute-done.24.refs_15_), channel_id=1, source_target_pairs={{0,1},{1,0},{2,3},{3,2},{4,5},{5,4},{6,7},{7,6},{8,9},{9,8},{10,11... | collective-permute-start | bytes 884744 | tf_op jit(solution)/shard_map/ppermute | solution.py:51
  114.9 18.8 %collective-permute-start.27 = (bf16[192,768]{1,0:T(8,128)(2,1)}, bf16[192,768]{1,0:T(8,128)(2,1)S(1)}, u32[]{:S(2)}, u32[]{:S(2)}) collective-permute-start(bf16[192,768]{1,0:T(8,128)(2,1)} %collective-permute-done.26.refs_17_), channel_id=1, source_target_pairs={{0,1},{1,0},{2,3},{3,2},{4,5},{5,4},{6,7},{7,6},{8,9},{9,8},{10,11... | collective-permute-start | bytes 884744 | tf_op jit(solution)/shard_map/ppermute | solution.py:51
  172.9 11.8 %collective-permute-start.30 = (f32[256,768]{1,0:T(8,128)S(1)}, f32[256,768]{1,0:T(8,128)S(1)}, u32[]{:S(2)}, u32[]{:S(2)}) collective-permute-start(f32[256,768]{1,0:T(8,128)S(1)} %get-tuple-element.96), channel_id=1, source_target_pairs={{0,8},{8,0},{16,24},{24,16},{1,9},{9,1},{17,25},{25,17},{2,10},{10... | collective-permute-start | bytes 2359304 | tf_op jit(solution)/shard_map/ppermute | solution.py:51
  177.4 59.8 %collective-permute-start.50 = (bf16[8,96,768]{2,1,0:T(8,128)(2,1)S(1)}, bf16[8,96,768]{2,1,0:T(8,128)(2,1)}, u32[]{:S(2)}, u32[]{:S(2)}) collective-permute-start(bf16[8,96,768]{2,1,0:T(8,128)(2,1)S(1)} %dynamic-slice_bitcast_fusion.1), channel_id=1, source_target_pairs={{0,16},{8,24},{16,0},{24,8},{1,17},{9,25},{17,1},{25,9},{2,18},{10... | collective-permute-start | bytes 3538952 | tf_op jit(solution)/shard_map/ppermute | solution.py:51
  193.9 13.0 %collective-permute-start.32 = (bf16[192,256]{1,0:T(8,128)(2,1)S(1)}, bf16[192,256]{1,0:T(8,128)(2,1)S(1)}, u32[]{:S(2)}, u32[]{:S(2)}) collective-permute-start(bf16[192,256]{1,0:T(8,128)(2,1)S(1)} %get-tuple-element.115), channel_id=1, source_target_pairs={{0,16},{8,24},{16,0},{24,8},{1,17},{9,25},{17,1},{25,9},{2,18},{10... | collective-permute-start | bytes 294920 | tf_op jit(solution)/shard_map/ppermute | solution.py:51
  194.2 15.2 %collective-permute-start.33 = (bf16[192,256]{1,0:T(8,128)(2,1)S(1)}, bf16[192,256]{1,0:T(8,128)(2,1)S(1)}, u32[]{:S(2)}, u32[]{:S(2)}) collective-permute-start(bf16[192,256]{1,0:T(8,128)(2,1)S(1)} %get-tuple-element.114), channel_id=1, source_target_pairs={{0,24},{8,16},{16,8},{24,0},{1,25},{9,17},{17,9},{25,1},{2,26},{10... | collective-permute-start | bytes 294920 | tf_op jit(solution)/shard_map/ppermute | solution.py:51
  198.5 55.6 %collective-permute-start.42 = (bf16[8,96,384]{2,1,0:T(8,128)(2,1)S(1)}, bf16[8,96,384]{2,1,0:T(8,128)(2,1)S(1)}, u32[]{:S(2)}, u32[]{:S(2)}) collective-permute-start(bf16[8,96,384]{2,1,0:T(8,128)(2,1)S(1)} %bitcast.211), channel_id=1, source_target_pairs={{0,8},{8,0},{16,24},{24,16},{1,9},{9,1},{17,25},{25,17},{2,10},{10... | collective-permute-start | bytes 1769480 | tf_op jit(solution)/shard_map/ppermute | solution.py:51
  235.4 13.9 %collective-permute-start.36 = (bf16[4,104,576]{2,1,0:T(8,128)(2,1)}, bf16[4,104,576]{2,1,0:T(8,128)(2,1)}, u32[]{:S(2)}, u32[]{:S(2)}) collective-permute-start(bf16[4,104,576]{2,1,0:T(8,128)(2,1)} %dynamic-slice_bitcast_fusion.4), channel_id=1, source_target_pairs={{0,1},{1,0},{2,3},{3,2},{4,5},{5,4},{6,7},{7,6},{8,9},{9,8},{10,11... | collective-permute-start | bytes 1437704 | tf_op jit(solution)/shard_map/ppermute | solution.py:51
  240.2 60.0 %collective-permute-start.51 = (bf16[4,96,768]{2,1,0:T(8,128)(2,1)}, bf16[4,96,768]{2,1,0:T(8,128)(2,1)}, u32[]{:S(2)}, u32[]{:S(2)}) collective-permute-start(bf16[4,96,768]{2,1,0:T(8,128)(2,1)} %dynamic-slice_bitcast_fusion.3), channel_id=1, source_target_pairs={{0,1},{1,0},{2,3},{3,2},{4,5},{5,4},{6,7},{7,6},{8,9},{9,8},{10,11... | collective-permute-start | bytes 1769480 | tf_op jit(solution)/shard_map/ppermute | solution.py:51
  255.9 60.3 %collective-permute-start.43 = (bf16[8,56,1920]{2,1,0:T(8,128)(2,1)}, bf16[8,56,1920]{2,1,0:T(8,128)(2,1)}, u32[]{:S(2)}, u32[]{:S(2)}) collective-permute-start(bf16[8,56,1920]{2,1,0:T(8,128)(2,1)} %dynamic-slice_bitcast_fusion), channel_id=1, source_target_pairs={{0,16},{8,24},{16,0},{24,8},{1,17},{9,25},{17,1},{25,9},{2,18},{10... | collective-permute-start | bytes 5160968 | tf_op jit(solution)/shard_map/ppermute | solution.py:51
  261.2 34.7 %collective-permute-start.40 = (bf16[104,576]{1,0:T(8,128)(2,1)}, bf16[104,576]{1,0:T(8,128)(2,1)}, u32[]{:S(2)}, u32[]{:S(2)}) collective-permute-start(bf16[104,576]{1,0:T(8,128)(2,1)} %fusion.27), channel_id=1, source_target_pairs={{0,16},{8,24},{16,0},{24,8},{1,17},{9,25},{17,1},{25,9},{2,18},{10... | collective-permute-start | bytes 359432 | tf_op jit(solution)/shard_map/ppermute | solution.py:51
  262.5 82.7 %collective-permute-start.34 = (f32[2,256,768]{2,1,0:T(8,128)}, f32[2,256,768]{2,1,0:T(8,128)}, u32[]{:S(2)}, u32[]{:S(2)}) collective-permute-start(f32[2,256,768]{2,1,0:T(8,128)} %get-tuple-element.83), channel_id=1, source_target_pairs={{0,8},{8,0},{16,24},{24,16},{1,9},{9,1},{17,25},{25,17},{2,10},{10... | collective-permute-start | bytes 4718600 | tf_op jit(solution)/shard_map/ppermute | solution.py:51
  318.2 19.1 %collective-permute-start.44 = (bf16[4,56,1920]{2,1,0:T(8,128)(2,1)S(1)}, bf16[4,56,1920]{2,1,0:T(8,128)(2,1)}, u32[]{:S(2)}, u32[]{:S(2)}) collective-permute-start(bf16[4,56,1920]{2,1,0:T(8,128)(2,1)S(1)} %dynamic-slice_bitcast_fusion.2), channel_id=1, source_target_pairs={{0,1},{1,0},{2,3},{3,2},{4,5},{5,4},{6,7},{7,6},{8,9},{9,8},{10,11... | collective-permute-start | bytes 2580488 | tf_op jit(solution)/shard_map/ppermute | solution.py:51
  343.9 13.4 %collective-permute-start.47 = (bf16[56,1920]{1,0:T(8,128)(2,1)S(1)}, bf16[56,1920]{1,0:T(8,128)(2,1)S(1)}, u32[]{:S(2)}, u32[]{:S(2)}) collective-permute-start(bf16[56,1920]{1,0:T(8,128)(2,1)S(1)} %get-tuple-element.103), channel_id=1, source_target_pairs={{0,6},{1,7},{2,4},{3,5},{4,2},{5,3},{6,0},{7,1},{8,14},{9,15},{10,... | collective-permute-start | bytes 645128 | tf_op jit(solution)/shard_map/ppermute | solution.py:51
  357.8 12.9 %collective-permute-start.35 = (bf16[256,768]{1,0:T(8,128)(2,1)S(1)}, bf16[256,768]{1,0:T(8,128)(2,1)S(1)}, u32[]{:S(2)}, u32[]{:S(2)}) collective-permute-start(bf16[256,768]{1,0:T(8,128)(2,1)S(1)} %fusion.18), channel_id=1, source_target_pairs={{0,16},{8,24},{16,0},{24,8},{1,17},{9,25},{17,1},{25,9},{2,18},{10... | collective-permute-start | bytes 1179656 | tf_op jit(solution)/shard_map/ppermute | solution.py:51
  (71 other events, 702.9 us)
